TPU v7x, 512 devices: a whole 4x4x16 slice. The times are simulated.
512 devices in a mesh: tm: 8 (over x, core), tile: 64 (over y, z).
Axes of the slice: x: 4, y: 4, z: 16, core: 2. Of those that a mesh axis runs over, the one named last changes fastest.
Arguments:
- starts: float32 [8, 98304, 128], P('tm', 'tile'), may hold values from -6 to 6
- sources: float32 [98304, 128], P('tile'), may hold values from -6 to 6
- fine_ops: float32 [8, 768, 4, 128, 128], P('tm', 'tile'), may hold values from -0.1875 to 0.1875
- col_index: int32 [8, 768, 4], P('tm', 'tile'), may hold values from 0 to 15, as said below
- live_count: int32 [8, 768], P('tm', 'tile'), may hold values from 1 to 4, as said below
- coarse_op: float32 [24576, 768], P('tile'), may hold values from -0.15625 to 0.15625
- cell_map: int32 [98304], P('tile'), may hold values from 0 to 383, as said below
Outputs:
- corrected: float32 [8, 98304, 128], P('tm', 'tile')
Inputs may be any that keep to these rules, and one draw needn't show every extreme that they name: `col_index`: each entry names one of the 16 blocks of a tile's fine window. Slots from live_count on are padding and carry no transport. `cell_map`: each entry is a local coarse index within its own tile; every coarse cell of every tile has at least one fine cell.
All inputs are finite; a program needn't handle non-finite values.
Results may differ from a plain program's by a relative error of at most 0.0003.
Values sent between devices are 32-bit elements; how exact they have to be, the bound alone decides.
No kernel may reach another device: no remote copies, remote signals or barrier semaphores. Data moves between devices by JAX's collectives and lax.ppermute only.
A program may use at most 64 MiB of HBM per device.

v0:
```python
import jax
import jax.numpy as jnp
from jax import lax
from jax.sharding import PartitionSpec as P

HALO = 256
STEPS = 2


def extended_2(cells, sides, width):
    for axis, dim in sides:
        count = lax.axis_size(axis)
        head = lax.slice_in_dim(cells, 0, width, axis=dim)
        tail = lax.slice_in_dim(cells, cells.shape[dim] - width, cells.shape[dim], axis=dim)
        cells = jnp.concatenate(
            [
                lax.ppermute(tail, axis, [(i, (i + 1) % count) for i in range(count)]),
                cells,
                lax.ppermute(head, axis, [((i + 1) % count, i) for i in range(count)]),
            ],
            axis=dim,
        )
    return cells


def passed_along(block, axis, distance):
    devices = range(lax.axis_size(axis))
    route = [(i - distance, i) for i in devices if i - distance in devices]
    return lax.ppermute(block, axis, route)


def on_device(starts, sources, fine_ops, col_index, live_count, coarse_op, cell_map):
    first_state = starts[0]
    transport = fine_ops[0]
    columns = col_index[0]
    slot_counts = live_count[0]
    row_count, tracers = first_state.shape
    slot_total = transport.shape[1]
    block_size = transport.shape[2]
    coarse = coarse_op.shape[0]
    coarse_rim = (coarse_op.shape[1] - coarse) // 2
    live_mask = (jnp.arange(slot_total)[None, :] < slot_counts[:, None]).astype(jnp.float32)
    fine_end = first_state
    for step_index in range(STEPS):
        fine_extended = extended_2(fine_end, (("tile", 0),), HALO)
        pieces = (
            fine_extended.reshape(-1, block_size, tracers)[columns] * live_mask[:, :, None, None]
        )
        transported = jnp.einsum(
            "bkij,bkjn->bin", transport, pieces, precision=lax.Precision.HIGHEST
        )
        fine_end = transported.reshape(row_count, tracers) + sources
    onehot = (cell_map[:, None] == jnp.arange(coarse, dtype=jnp.int32)[None, :]).astype(jnp.float32)
    children = jnp.sum(onehot, axis=0)
    following = passed_along(first_state, "tm", -1)
    sums = lax.dot_general(
        onehot, fine_end - following, (((0,), (0,)), ((), ())), precision=lax.Precision.HIGHEST
    )
    jump_term = sums / children[:, None]

    def coarse_apply(coarse_state):
        extended = extended_2(coarse_state, (("tile", 0),), coarse_rim)
        return jnp.dot(coarse_op, extended, precision=lax.Precision.HIGHEST)

    slice_count = lax.axis_size("tm")
    empty_coarse = jnp.zeros((coarse, tracers), jnp.float32)

    def advance(step_index, current):
        return passed_along(coarse_apply(current) + jump_term, "tm", 1)

    current = lax.fori_loop(0, slice_count - 1, advance, empty_coarse)
    carried = coarse_apply(current)
    result = fine_end + jnp.dot(onehot, carried, precision=lax.Precision.HIGHEST)
    return result[None]


def solution(mesh):
    placed = (
        P("tm", "tile", None),
        P("tile", None),
        P("tm", "tile", None, None, None),
        P("tm", "tile", None),
        P("tm", "tile"),
        P("tile", None),
        P("tile"),
    )
    return jax.shard_map(
        on_device, mesh=mesh, in_specs=placed, out_specs=P("tm", "tile", None), check_vma=False
    )
```

profile of v0, /device:TPU:6, one launch (start us, length us, event | category | flops | bytes accessed | tf_op | source)
XLA Modules:
  0.0 243.3 jit_solution(16193968734345541092)
XLA Ops:
  1.8 3.8 %collective-permute-start.3 = (f32[256,128]{1,0:T(8,128)}, f32[256,128]{1,0:T(8,128)S(1)}, u32[]{:S(2)}, u32[]{:S(2)}) collective-permute-start(f32[256,128]{1,0:T(8,128)} %get-tuple-element.52), channel_id=1, source_target_pairs={{0,1},{1,2},{2,3},{3,4},{4,5},{5,6},{6,7},{7,8},{8,9},{9,10},{10,1... | collective-permute-start | bytes 393224 | tf_op jit(solution)/shard_map/ppermute | solution.py:17
  5.6 11.9 %collective-permute-start.4 = (f32[256,128]{1,0:T(8,128)S(1)}, f32[256,128]{1,0:T(8,128)S(1)}, u32[]{:S(2)}, u32[]{:S(2)}) collective-permute-start(f32[256,128]{1,0:T(8,128)S(1)} %get-tuple-element.53), channel_id=1, source_target_pairs={{1,0},{2,1},{3,2},{4,3},{5,4},{6,5},{7,6},{8,7},{9,8},{10,9},{11,1... | collective-permute-start | bytes 393224 | tf_op jit(solution)/shard_map/ppermute | solution.py:19
  17.6 1.9 collective-permute-start.7
  22.4 2.2 pad_maximum_fusion
  24.6 3.6 %gather_fusion = f32[48,128,128]{2,1,0:T(8,128)} fusion(f32[16,128,128]{2,1,0:T(8,128)} %bitcast.47, s32[1024]{0:T(1024)S(1)} %pad_clamp_fusion), kind=kCustom, calls=%fused_computation | custom fusion | bytes 6291648 | tf_op jit(solution)/shard_map/gather | solution.py:47
  28.2 5.6 %fusion.9 = f32[12,128,128,1]{1,2,3,0:T(8,128)S(1)} fusion(f32[1,12,4,128,128]{4,3,2,1,0:T(8,128)S(1)} %copy-done, f32[12,4,128,128]{3,2,1,0:T(8,128)} %bitcast.49, f32[12,4]{1,0:T(8,128)S(1)} %fusion.27), kind=kOutput, calls=%fused_computation.12 | convolution fusion | flops 1208745984 | bytes 7078080 | tf_op jit(solution)/shard_map/bkij,bkjn->bin/dot_general | solution.py:49
  34.0 1.9 collective-permute-start.5
  35.9 7.4 %collective-permute-start.6 = (f32[256,128]{1,0:T(8,128)S(1)}, f32[256,128]{1,0:T(8,128)S(1)}, u32[]{:S(2)}, u32[]{:S(2)}) collective-permute-start(f32[256,128]{1,0:T(8,128)S(1)} %get-tuple-element.51), channel_id=1, source_target_pairs={{1,0},{2,1},{3,2},{4,3},{5,4},{6,5},{7,6},{8,7},{9,8},{10,9},{11,1... | collective-permute-start | bytes 393224 | tf_op jit(solution)/shard_map/ppermute | solution.py:19
  48.0 3.6 %gather_fusion.1 = f32[48,128,128]{2,1,0:T(8,128)} fusion(f32[16,128,128]{2,1,0:T(8,128)} %bitcast.46, s32[1024]{0:T(1024)S(1)} %pad_clamp_fusion), kind=kCustom, calls=%fused_computation.1 | custom fusion | bytes 6291648 | tf_op jit(solution)/shard_map/gather | solution.py:47
  51.6 5.6 %fusion.7 = f32[12,128,128,1]{1,2,3,0:T(8,128)S(1)} fusion(f32[1,12,4,128,128]{4,3,2,1,0:T(8,128)S(1)} %copy-done, f32[12,4,128,128]{3,2,1,0:T(8,128)} %bitcast.48, f32[12,4]{1,0:T(8,128)S(1)} %fusion.27), kind=kOutput, calls=%fused_computation.10 | convolution fusion | flops 1208745984 | bytes 7078080 | tf_op jit(solution)/shard_map/bkij,bkjn->bin/dot_general | solution.py:49
  58.2 3.4 %fusion.19 = f32[384,128]{1,0:T(8,128)S(1)} fusion(s32[1536]{0:T(1024)S(1)} %copy-done.4, f32[1536,128]{1,0:T(8,128)S(1)} %bitcast_add_fusion, f32[1536,128]{1,0:T(8,128)} %collective-permute-done.7, f32[384]{0:T(512)S(1)} %convert_reduce_fusion), kind=kOutput, calls=%fused_computation.25 | convolution fusion | flops 906805248 | bytes 1777152 | tf_op jit(solution)/shard_map/dot_general | solution.py:56
  61.8 164.0 %while.10 = (s32[]{:T(128)}, f32[384,128]{0,1:T(8,128)S(1)}, f32[384,768]{1,0:T(8,128)}, f32[384,128]{0,1:T(8,128)S(1)}, s32[]{:T(128)}) while((s32[]{:T(128)}, f32[384,128]{0,1:T(8,128)S(1)}, f32[384,768]{1,0:T(8,128)}, f32[384,128]{0,1:T(8,128)S(1)}, s32[]{:T(128)}) %tuple.27), condition=%wide.region_2.0_spmd, body=%wide.region_1.0_spmd.sunk | while | flops 453230592 | bytes 3932341 | solution.py:71
  61.9 7.7 %collective-permute-start = (f32[192,128]{0,1:T(8,128)S(1)}, f32[192,128]{0,1:T(8,128)S(1)}, u32[]{:S(2)}, u32[]{:S(2)}) collective-permute-start(f32[192,128]{0,1:T(8,128)S(1)} %get-tuple-element.83), channel_id=1, source_target_pairs={{1,0},{2,1},{3,2},{4,3},{5,4},{6,5},{7,6},{8,7},{9,8},{10,9},{11,1... | collective-permute-start | bytes 294920 | tf_op jit(solution)/shard_map/while/body/eval_jaxpr/ppermute | solution.py:19
  69.6 1.9 collective-permute-start.1
  72.7 7.4 %collective-permute-done.1 = f32[192,128]{0,1:T(8,128)S(1)} collective-permute-done((f32[192,128]{0,1:T(8,128)S(1)}, f32[192,128]{0,1:T(8,128)S(1)}, u32[]{:S(2)}, u32[]{:S(2)}) %collective-permute-start.1) | collective-permute-done | bytes 98336 | tf_op jit(solution)/shard_map/while/body/eval_jaxpr/ppermute | solution.py:17
  80.1 3.2 %fusion.42 = f32[384,128]{0,1:T(8,128)} fusion(f32[384,128]{0,1:T(8,128)S(1)} %get-tuple-element.98, f32[384,768]{1,0:T(8,128)} %get-tuple-element.97, f32[192,128]{0,1:T(8,128)S(1)} %collective-permute-done, f32[384,128]{0,1:T(8,128)S(1)} %get-tuple-element.91, f32[192,128]{0,1:T(8,128)S(1)} %collective-permute-done.1), kind=kOutput, calls=%fused_computation.3.clone.1 | convolution fusion | flops 453230592 | bytes 1966080 | tf_op jit(solution)/shard_map/while/body/eval_jaxpr/dot_general | solution.py:63
  85.2 5.3 %collective-permute-done.2 = f32[384,128]{0,1:T(8,128)S(1)} collective-permute-done((f32[384,128]{0,1:T(8,128)}, f32[384,128]{0,1:T(8,128)S(1)}, u32[]{:S(2)}, u32[]{:S(2)}) %collective-permute-start.2) | collective-permute-done | bytes 196640 | tf_op jit(solution)/shard_map/while/body/eval_jaxpr/ppermute | solution.py:29
  92.5 3.9 %collective-permute-start.1 = (f32[192,128]{0,1:T(8,128)S(1)}, f32[192,128]{0,1:T(8,128)S(1)}, u32[]{:S(2)}, u32[]{:S(2)}) collective-permute-start(f32[192,128]{0,1:T(8,128)S(1)} %get-tuple-element.84), channel_id=1, source_target_pairs={{0,1},{1,2},{2,3},{3,4},{4,5},{5,6},{6,7},{7,8},{8,9},{9,10},{10,1... | collective-permute-start | bytes 294920 | tf_op jit(solution)/shard_map/while/body/eval_jaxpr/ppermute | solution.py:17
  97.4 5.2 %collective-permute-done.1 = f32[192,128]{0,1:T(8,128)S(1)} collective-permute-done((f32[192,128]{0,1:T(8,128)S(1)}, f32[192,128]{0,1:T(8,128)S(1)}, u32[]{:S(2)}, u32[]{:S(2)}) %collective-permute-start.1) | collective-permute-done | bytes 98336 | tf_op jit(solution)/shard_map/while/body/eval_jaxpr/ppermute | solution.py:17
  102.7 3.2 %fusion.42 = f32[384,128]{0,1:T(8,128)} fusion(f32[384,128]{0,1:T(8,128)S(1)} %get-tuple-element.98, f32[384,768]{1,0:T(8,128)} %get-tuple-element.97, f32[192,128]{0,1:T(8,128)S(1)} %collective-permute-done, f32[384,128]{0,1:T(8,128)S(1)} %get-tuple-element.91, f32[192,128]{0,1:T(8,128)S(1)} %collective-permute-done.1), kind=kOutput, calls=%fused_computation.3.clone.1 | convolution fusion | flops 453230592 | bytes 1966080 | tf_op jit(solution)/shard_map/while/body/eval_jaxpr/dot_general | solution.py:63
  107.7 5.3 %collective-permute-done.2 = f32[384,128]{0,1:T(8,128)S(1)} collective-permute-done((f32[384,128]{0,1:T(8,128)}, f32[384,128]{0,1:T(8,128)S(1)}, u32[]{:S(2)}, u32[]{:S(2)}) %collective-permute-start.2) | collective-permute-done | bytes 196640 | tf_op jit(solution)/shard_map/while/body/eval_jaxpr/ppermute | solution.py:29
  115.0 3.9 %collective-permute-start.1 = (f32[192,128]{0,1:T(8,128)S(1)}, f32[192,128]{0,1:T(8,128)S(1)}, u32[]{:S(2)}, u32[]{:S(2)}) collective-permute-start(f32[192,128]{0,1:T(8,128)S(1)} %get-tuple-element.84), channel_id=1, source_target_pairs={{0,1},{1,2},{2,3},{3,4},{4,5},{5,6},{6,7},{7,8},{8,9},{9,10},{10,1... | collective-permute-start | bytes 294920 | tf_op jit(solution)/shard_map/while/body/eval_jaxpr/ppermute | solution.py:17
  120.0 5.2 %collective-permute-done.1 = f32[192,128]{0,1:T(8,128)S(1)} collective-permute-done((f32[192,128]{0,1:T(8,128)S(1)}, f32[192,128]{0,1:T(8,128)S(1)}, u32[]{:S(2)}, u32[]{:S(2)}) %collective-permute-start.1) | collective-permute-done | bytes 98336 | tf_op jit(solution)/shard_map/while/body/eval_jaxpr/ppermute | solution.py:17
  125.2 3.2 %fusion.42 = f32[384,128]{0,1:T(8,128)} fusion(f32[384,128]{0,1:T(8,128)S(1)} %get-tuple-element.98, f32[384,768]{1,0:T(8,128)} %get-tuple-element.97, f32[192,128]{0,1:T(8,128)S(1)} %collective-permute-done, f32[384,128]{0,1:T(8,128)S(1)} %get-tuple-element.91, f32[192,128]{0,1:T(8,128)S(1)} %collective-permute-done.1), kind=kOutput, calls=%fused_computation.3.clone.1 | convolution fusion | flops 453230592 | bytes 1966080 | tf_op jit(solution)/shard_map/while/body/eval_jaxpr/dot_general | solution.py:63
  130.3 5.3 %collective-permute-done.2 = f32[384,128]{0,1:T(8,128)S(1)} collective-permute-done((f32[384,128]{0,1:T(8,128)}, f32[384,128]{0,1:T(8,128)S(1)}, u32[]{:S(2)}, u32[]{:S(2)}) %collective-permute-start.2) | collective-permute-done | bytes 196640 | tf_op jit(solution)/shard_map/while/body/eval_jaxpr/ppermute | solution.py:29
  135.7 1.9 collective-permute-start
  137.6 3.9 %collective-permute-start.1 = (f32[192,128]{0,1:T(8,128)S(1)}, f32[192,128]{0,1:T(8,128)S(1)}, u32[]{:S(2)}, u32[]{:S(2)}) collective-permute-start(f32[192,128]{0,1:T(8,128)S(1)} %get-tuple-element.84), channel_id=1, source_target_pairs={{0,1},{1,2},{2,3},{3,4},{4,5},{5,6},{6,7},{7,8},{8,9},{9,10},{10,1... | collective-permute-start | bytes 294920 | tf_op jit(solution)/shard_map/while/body/eval_jaxpr/ppermute | solution.py:17
  142.5 5.2 %collective-permute-done.1 = f32[192,128]{0,1:T(8,128)S(1)} collective-permute-done((f32[192,128]{0,1:T(8,128)S(1)}, f32[192,128]{0,1:T(8,128)S(1)}, u32[]{:S(2)}, u32[]{:S(2)}) %collective-permute-start.1) | collective-permute-done | bytes 98336 | tf_op jit(solution)/shard_map/while/body/eval_jaxpr/ppermute | solution.py:17
  147.8 3.2 %fusion.42 = f32[384,128]{0,1:T(8,128)} fusion(f32[384,128]{0,1:T(8,128)S(1)} %get-tuple-element.98, f32[384,768]{1,0:T(8,128)} %get-tuple-element.97, f32[192,128]{0,1:T(8,128)S(1)} %collective-permute-done, f32[384,128]{0,1:T(8,128)S(1)} %get-tuple-element.91, f32[192,128]{0,1:T(8,128)S(1)} %collective-permute-done.1), kind=kOutput, calls=%fused_computation.3.clone.1 | convolution fusion | flops 453230592 | bytes 1966080 | tf_op jit(solution)/shard_map/while/body/eval_jaxpr/dot_general | solution.py:63
  152.9 5.3 %collective-permute-done.2 = f32[384,128]{0,1:T(8,128)S(1)} collective-permute-done((f32[384,128]{0,1:T(8,128)}, f32[384,128]{0,1:T(8,128)S(1)}, u32[]{:S(2)}, u32[]{:S(2)}) %collective-permute-start.2) | collective-permute-done | bytes 196640 | tf_op jit(solution)/shard_map/while/body/eval_jaxpr/ppermute | solution.py:29
  158.2 1.9 collective-permute-start
  160.2 3.9 %collective-permute-start.1 = (f32[192,128]{0,1:T(8,128)S(1)}, f32[192,128]{0,1:T(8,128)S(1)}, u32[]{:S(2)}, u32[]{:S(2)}) collective-permute-start(f32[192,128]{0,1:T(8,128)S(1)} %get-tuple-element.84), channel_id=1, source_target_pairs={{0,1},{1,2},{2,3},{3,4},{4,5},{5,6},{6,7},{7,8},{8,9},{9,10},{10,1... | collective-permute-start | bytes 294920 | tf_op jit(solution)/shard_map/while/body/eval_jaxpr/ppermute | solution.py:17
  165.1 5.2 %collective-permute-done.1 = f32[192,128]{0,1:T(8,128)S(1)} collective-permute-done((f32[192,128]{0,1:T(8,128)S(1)}, f32[192,128]{0,1:T(8,128)S(1)}, u32[]{:S(2)}, u32[]{:S(2)}) %collective-permute-start.1) | collective-permute-done | bytes 98336 | tf_op jit(solution)/shard_map/while/body/eval_jaxpr/ppermute | solution.py:17
  170.4 3.2 %fusion.42 = f32[384,128]{0,1:T(8,128)} fusion(f32[384,128]{0,1:T(8,128)S(1)} %get-tuple-element.98, f32[384,768]{1,0:T(8,128)} %get-tuple-element.97, f32[192,128]{0,1:T(8,128)S(1)} %collective-permute-done, f32[384,128]{0,1:T(8,128)S(1)} %get-tuple-element.91, f32[192,128]{0,1:T(8,128)S(1)} %collective-permute-done.1), kind=kOutput, calls=%fused_computation.3.clone.1 | convolution fusion | flops 453230592 | bytes 1966080 | tf_op jit(solution)/shard_map/while/body/eval_jaxpr/dot_general | solution.py:63
  175.5 5.3 %collective-permute-done.2 = f32[384,128]{0,1:T(8,128)S(1)} collective-permute-done((f32[384,128]{0,1:T(8,128)}, f32[384,128]{0,1:T(8,128)S(1)}, u32[]{:S(2)}, u32[]{:S(2)}) %collective-permute-start.2) | collective-permute-done | bytes 196640 | tf_op jit(solution)/shard_map/while/body/eval_jaxpr/ppermute | solution.py:29
  180.8 1.9 collective-permute-start
  182.7 3.9 %collective-permute-start.1 = (f32[192,128]{0,1:T(8,128)S(1)}, f32[192,128]{0,1:T(8,128)S(1)}, u32[]{:S(2)}, u32[]{:S(2)}) collective-permute-start(f32[192,128]{0,1:T(8,128)S(1)} %get-tuple-element.84), channel_id=1, source_target_pairs={{0,1},{1,2},{2,3},{3,4},{4,5},{5,6},{6,7},{7,8},{8,9},{9,10},{10,1... | collective-permute-start | bytes 294920 | tf_op jit(solution)/shard_map/while/body/eval_jaxpr/ppermute | solution.py:17
  187.7 5.2 %collective-permute-done.1 = f32[192,128]{0,1:T(8,128)S(1)} collective-permute-done((f32[192,128]{0,1:T(8,128)S(1)}, f32[192,128]{0,1:T(8,128)S(1)}, u32[]{:S(2)}, u32[]{:S(2)}) %collective-permute-start.1) | collective-permute-done | bytes 98336 | tf_op jit(solution)/shard_map/while/body/eval_jaxpr/ppermute | solution.py:17
  192.9 3.2 %fusion.42 = f32[384,128]{0,1:T(8,128)} fusion(f32[384,128]{0,1:T(8,128)S(1)} %get-tuple-element.98, f32[384,768]{1,0:T(8,128)} %get-tuple-element.97, f32[192,128]{0,1:T(8,128)S(1)} %collective-permute-done, f32[384,128]{0,1:T(8,128)S(1)} %get-tuple-element.91, f32[192,128]{0,1:T(8,128)S(1)} %collective-permute-done.1), kind=kOutput, calls=%fused_computation.3.clone.1 | convolution fusion | flops 453230592 | bytes 1966080 | tf_op jit(solution)/shard_map/while/body/eval_jaxpr/dot_general | solution.py:63
  198.0 5.3 %collective-permute-done.2 = f32[384,128]{0,1:T(8,128)S(1)} collective-permute-done((f32[384,128]{0,1:T(8,128)}, f32[384,128]{0,1:T(8,128)S(1)}, u32[]{:S(2)}, u32[]{:S(2)}) %collective-permute-start.2) | collective-permute-done | bytes 196640 | tf_op jit(solution)/shard_map/while/body/eval_jaxpr/ppermute | solution.py:29
  203.4 1.9 collective-permute-start
  205.3 3.9 %collective-permute-start.1 = (f32[192,128]{0,1:T(8,128)S(1)}, f32[192,128]{0,1:T(8,128)S(1)}, u32[]{:S(2)}, u32[]{:S(2)}) collective-permute-start(f32[192,128]{0,1:T(8,128)S(1)} %get-tuple-element.84), channel_id=1, source_target_pairs={{0,1},{1,2},{2,3},{3,4},{4,5},{5,6},{6,7},{7,8},{8,9},{9,10},{10,1... | collective-permute-start | bytes 294920 | tf_op jit(solution)/shard_map/while/body/eval_jaxpr/ppermute | solution.py:17
  210.2 5.2 %collective-permute-done.1 = f32[192,128]{0,1:T(8,128)S(1)} collective-permute-done((f32[192,128]{0,1:T(8,128)S(1)}, f32[192,128]{0,1:T(8,128)S(1)}, u32[]{:S(2)}, u32[]{:S(2)}) %collective-permute-start.1) | collective-permute-done | bytes 98336 | tf_op jit(solution)/shard_map/while/body/eval_jaxpr/ppermute | solution.py:17
  215.5 3.2 %fusion.42 = f32[384,128]{0,1:T(8,128)} fusion(f32[384,128]{0,1:T(8,128)S(1)} %get-tuple-element.98, f32[384,768]{1,0:T(8,128)} %get-tuple-element.97, f32[192,128]{0,1:T(8,128)S(1)} %collective-permute-done, f32[384,128]{0,1:T(8,128)S(1)} %get-tuple-element.91, f32[192,128]{0,1:T(8,128)S(1)} %collective-permute-done.1), kind=kOutput, calls=%fused_computation.3.clone.1 | convolution fusion | flops 453230592 | bytes 1966080 | tf_op jit(solution)/shard_map/while/body/eval_jaxpr/dot_general | solution.py:63
  220.6 5.3 %collective-permute-done.2 = f32[384,128]{0,1:T(8,128)S(1)} collective-permute-done((f32[384,128]{0,1:T(8,128)}, f32[384,128]{0,1:T(8,128)S(1)}, u32[]{:S(2)}, u32[]{:S(2)}) %collective-permute-start.2) | collective-permute-done | bytes 196640 | tf_op jit(solution)/shard_map/while/body/eval_jaxpr/ppermute | solution.py:29
  227.9 7.2 %collective-permute-start.9 = (f32[192,128]{0,1:T(8,128)S(1)}, f32[192,128]{0,1:T(8,128)S(1)}, u32[]{:S(2)}, u32[]{:S(2)}) collective-permute-start(f32[192,128]{0,1:T(8,128)S(1)} %get-tuple-element.55), channel_id=1, source_target_pairs={{1,0},{2,1},{3,2},{4,3},{5,4},{6,5},{7,6},{8,7},{9,8},{10,9},{11,1... | collective-permute-start | bytes 294920 | tf_op jit(solution)/shard_map/ppermute | solution.py:19
  237.6 2.5 %fusion.21 = f32[128,384]{1,0:T(8,128)S(1)} fusion(f32[384,768]{1,0:T(8,128)} %get-tuple-element.101, f32[192,128]{0,1:T(8,128)S(1)} %collective-permute-done.9, f32[384,128]{0,1:T(8,128)S(1)} %get-tuple-element.27, f32[192,128]{0,1:T(8,128)S(1)} %collective-permute-done.8), kind=kOutput, calls=%fused_computation.31 | convolution fusion | flops 453181440 | bytes 1769472 | tf_op jit(solution)/shard_map/dot_general | solution.py:63
  240.1 3.2 %fusion.13 = f32[1,1536,128]{2,1,0:T(8,128)} fusion(f32[1536,128]{1,0:T(8,128)} %copy-done.1, f32[128,384]{1,0:T(8,128)S(1)} %fusion.21, s32[1536]{0:T(1024)S(1)} %copy-done.5), kind=kOutput, calls=%fused_computation.17 | convolution fusion | flops 906756096 | bytes 1775616 | tf_op jit(solution)/shard_map/dot_general | solution.py:73
  (57 shorter events, 39.9 us)
Async XLA Ops:
  0.0 28.2 %copy-start = (f32[1,12,4,128,128]{4,3,2,1,0:T(8,128)S(1)}, f32[1,12,4,128,128]{4,3,2,1,0:T(8,128)}, u32[]{:S(2)}) copy-start(f32[1,12,4,128,128]{4,3,2,1,0:T(8,128)} %param.11) | copy-start | bytes 9437188
  1.8 20.6 %collective-permute-start.3 = (f32[256,128]{1,0:T(8,128)}, f32[256,128]{1,0:T(8,128)S(1)}, u32[]{:S(2)}, u32[]{:S(2)}) collective-permute-start(f32[256,128]{1,0:T(8,128)} %get-tuple-element.52), channel_id=1, source_target_pairs={{0,1},{1,2},{2,3},{3,4},{4,5},{5,6},{6,7},{7,8},{8,9},{9,10},{10,1... | collective-permute-start | bytes 393224 | tf_op jit(solution)/shard_map/ppermute | solution.py:17
  5.6 16.8 %collective-permute-start.4 = (f32[256,128]{1,0:T(8,128)S(1)}, f32[256,128]{1,0:T(8,128)S(1)}, u32[]{:S(2)}, u32[]{:S(2)}) collective-permute-start(f32[256,128]{1,0:T(8,128)S(1)} %get-tuple-element.53), channel_id=1, source_target_pairs={{1,0},{2,1},{3,2},{4,3},{5,4},{6,5},{7,6},{8,7},{9,8},{10,9},{11,1... | collective-permute-start | bytes 393224 | tf_op jit(solution)/shard_map/ppermute | solution.py:19
  17.6 39.8 %collective-permute-start.7 = (f32[1536,128]{1,0:T(8,128)}, f32[1536,128]{1,0:T(8,128)}, u32[]{:S(2)}, u32[]{:S(2)}) collective-permute-start(f32[1536,128]{1,0:T(8,128)} %bitcast.50), channel_id=1, source_target_pairs={{64,0},{128,64},{192,128},{256,192},{320,256},{384,320},{448,384},... | collective-permute-start | bytes 2359304 | tf_op jit(solution)/shard_map/ppermute | solution.py:29
  28.2 5.7 %copy-start.2 = (f32[1536,128]{1,0:T(8,128)S(1)}, f32[1536,128]{1,0:T(8,128)}, u32[]{:S(2)}) copy-start(f32[1536,128]{1,0:T(8,128)} %param.10) | copy-start | bytes 2359300
  28.2 15.1 %copy-start.4 = (s32[1536]{0:T(1024)S(1)}, s32[1536]{0:T(1024)}, u32[]{:S(2)}) copy-start(s32[1536]{0:T(1024)} %param.15) | copy-start | bytes 18436
  34.0 11.2 %collective-permute-start.5 = (f32[256,128]{1,0:T(8,128)S(1)}, f32[256,128]{1,0:T(8,128)S(1)}, u32[]{:S(2)}, u32[]{:S(2)}) collective-permute-start(f32[256,128]{1,0:T(8,128)S(1)} %get-tuple-element.50), channel_id=1, source_target_pairs={{0,1},{1,2},{2,3},{3,4},{4,5},{5,6},{6,7},{7,8},{8,9},{9,10},{10,1... | collective-permute-start | bytes 393224 | tf_op jit(solution)/shard_map/ppermute | solution.py:17
  35.9 11.0 %collective-permute-start.6 = (f32[256,128]{1,0:T(8,128)S(1)}, f32[256,128]{1,0:T(8,128)S(1)}, u32[]{:S(2)}, u32[]{:S(2)}) collective-permute-start(f32[256,128]{1,0:T(8,128)S(1)} %get-tuple-element.51), channel_id=1, source_target_pairs={{1,0},{2,1},{3,2},{4,3},{5,4},{6,5},{7,6},{8,7},{9,8},{10,9},{11,1... | collective-permute-start | bytes 393224 | tf_op jit(solution)/shard_map/ppermute | solution.py:19
  51.6 5.7 %copy-start.3 = (f32[1536,128]{1,0:T(8,128)S(1)}, f32[1536,128]{1,0:T(8,128)}, u32[]{:S(2)}) copy-start(f32[1536,128]{1,0:T(8,128)} %param.10) | copy-start | bytes 2359300
  57.4 0.9 copy-start.1
  61.8 178.3 %copy-start.5 = (s32[1536]{0:T(1024)S(1)}, s32[1536]{0:T(1024)}, u32[]{:S(2)}) copy-start(s32[1536]{0:T(1024)} %param.15) | copy-start | bytes 18436
  61.9 10.7 %collective-permute-start = (f32[192,128]{0,1:T(8,128)S(1)}, f32[192,128]{0,1:T(8,128)S(1)}, u32[]{:S(2)}, u32[]{:S(2)}) collective-permute-start(f32[192,128]{0,1:T(8,128)S(1)} %get-tuple-element.83), channel_id=1, source_target_pairs={{1,0},{2,1},{3,2},{4,3},{5,4},{6,5},{7,6},{8,7},{9,8},{10,9},{11,1... | collective-permute-start | bytes 294920 | tf_op jit(solution)/shard_map/while/body/eval_jaxpr/ppermute | solution.py:19
  69.6 10.4 %collective-permute-start.1 = (f32[192,128]{0,1:T(8,128)S(1)}, f32[192,128]{0,1:T(8,128)S(1)}, u32[]{:S(2)}, u32[]{:S(2)}) collective-permute-start(f32[192,128]{0,1:T(8,128)S(1)} %get-tuple-element.84), channel_id=1, source_target_pairs={{0,1},{1,2},{2,3},{3,4},{4,5},{5,6},{6,7},{7,8},{8,9},{9,10},{10,1... | collective-permute-start | bytes 294920 | tf_op jit(solution)/shard_map/while/body/eval_jaxpr/ppermute | solution.py:17
  83.3 7.2 %collective-permute-start.2 = (f32[384,128]{0,1:T(8,128)}, f32[384,128]{0,1:T(8,128)S(1)}, u32[]{:S(2)}, u32[]{:S(2)}) collective-permute-start(f32[384,128]{0,1:T(8,128)} %fusion.42), channel_id=1, source_target_pairs={{0,64},{64,128},{128,192},{192,256},{256,320},{320,384},{384,448},... | collective-permute-start | bytes 589832 | tf_op jit(solution)/shard_map/while/body/eval_jaxpr/ppermute | solution.py:29
  90.5 6.9 %collective-permute-start = (f32[192,128]{0,1:T(8,128)S(1)}, f32[192,128]{0,1:T(8,128)S(1)}, u32[]{:S(2)}, u32[]{:S(2)}) collective-permute-start(f32[192,128]{0,1:T(8,128)S(1)} %get-tuple-element.83), channel_id=1, source_target_pairs={{1,0},{2,1},{3,2},{4,3},{5,4},{6,5},{7,6},{8,7},{9,8},{10,9},{11,1... | collective-permute-start | bytes 294920 | tf_op jit(solution)/shard_map/while/body/eval_jaxpr/ppermute | solution.py:19
  92.5 10.2 %collective-permute-start.1 = (f32[192,128]{0,1:T(8,128)S(1)}, f32[192,128]{0,1:T(8,128)S(1)}, u32[]{:S(2)}, u32[]{:S(2)}) collective-permute-start(f32[192,128]{0,1:T(8,128)S(1)} %get-tuple-element.84), channel_id=1, source_target_pairs={{0,1},{1,2},{2,3},{3,4},{4,5},{5,6},{6,7},{7,8},{8,9},{9,10},{10,1... | collective-permute-start | bytes 294920 | tf_op jit(solution)/shard_map/while/body/eval_jaxpr/ppermute | solution.py:17
  105.8 7.2 %collective-permute-start.2 = (f32[384,128]{0,1:T(8,128)}, f32[384,128]{0,1:T(8,128)S(1)}, u32[]{:S(2)}, u32[]{:S(2)}) collective-permute-start(f32[384,128]{0,1:T(8,128)} %fusion.42), channel_id=1, source_target_pairs={{0,64},{64,128},{128,192},{192,256},{256,320},{320,384},{384,448},... | collective-permute-start | bytes 589832 | tf_op jit(solution)/shard_map/while/body/eval_jaxpr/ppermute | solution.py:29
  113.1 6.9 %collective-permute-start = (f32[192,128]{0,1:T(8,128)S(1)}, f32[192,128]{0,1:T(8,128)S(1)}, u32[]{:S(2)}, u32[]{:S(2)}) collective-permute-start(f32[192,128]{0,1:T(8,128)S(1)} %get-tuple-element.83), channel_id=1, source_target_pairs={{1,0},{2,1},{3,2},{4,3},{5,4},{6,5},{7,6},{8,7},{9,8},{10,9},{11,1... | collective-permute-start | bytes 294920 | tf_op jit(solution)/shard_map/while/body/eval_jaxpr/ppermute | solution.py:19
  115.0 10.2 %collective-permute-start.1 = (f32[192,128]{0,1:T(8,128)S(1)}, f32[192,128]{0,1:T(8,128)S(1)}, u32[]{:S(2)}, u32[]{:S(2)}) collective-permute-start(f32[192,128]{0,1:T(8,128)S(1)} %get-tuple-element.84), channel_id=1, source_target_pairs={{0,1},{1,2},{2,3},{3,4},{4,5},{5,6},{6,7},{7,8},{8,9},{9,10},{10,1... | collective-permute-start | bytes 294920 | tf_op jit(solution)/shard_map/while/body/eval_jaxpr/ppermute | solution.py:17
  128.4 7.2 %collective-permute-start.2 = (f32[384,128]{0,1:T(8,128)}, f32[384,128]{0,1:T(8,128)S(1)}, u32[]{:S(2)}, u32[]{:S(2)}) collective-permute-start(f32[384,128]{0,1:T(8,128)} %fusion.42), channel_id=1, source_target_pairs={{0,64},{64,128},{128,192},{192,256},{256,320},{320,384},{384,448},... | collective-permute-start | bytes 589832 | tf_op jit(solution)/shard_map/while/body/eval_jaxpr/ppermute | solution.py:29
  135.7 6.9 %collective-permute-start = (f32[192,128]{0,1:T(8,128)S(1)}, f32[192,128]{0,1:T(8,128)S(1)}, u32[]{:S(2)}, u32[]{:S(2)}) collective-permute-start(f32[192,128]{0,1:T(8,128)S(1)} %get-tuple-element.83), channel_id=1, source_target_pairs={{1,0},{2,1},{3,2},{4,3},{5,4},{6,5},{7,6},{8,7},{9,8},{10,9},{11,1... | collective-permute-start | bytes 294920 | tf_op jit(solution)/shard_map/while/body/eval_jaxpr/ppermute | solution.py:19
  137.6 10.2 %collective-permute-start.1 = (f32[192,128]{0,1:T(8,128)S(1)}, f32[192,128]{0,1:T(8,128)S(1)}, u32[]{:S(2)}, u32[]{:S(2)}) collective-permute-start(f32[192,128]{0,1:T(8,128)S(1)} %get-tuple-element.84), channel_id=1, source_target_pairs={{0,1},{1,2},{2,3},{3,4},{4,5},{5,6},{6,7},{7,8},{8,9},{9,10},{10,1... | collective-permute-start | bytes 294920 | tf_op jit(solution)/shard_map/while/body/eval_jaxpr/ppermute | solution.py:17
  151.0 7.2 %collective-permute-start.2 = (f32[384,128]{0,1:T(8,128)}, f32[384,128]{0,1:T(8,128)S(1)}, u32[]{:S(2)}, u32[]{:S(2)}) collective-permute-start(f32[384,128]{0,1:T(8,128)} %fusion.42), channel_id=1, source_target_pairs={{0,64},{64,128},{128,192},{192,256},{256,320},{320,384},{384,448},... | collective-permute-start | bytes 589832 | tf_op jit(solution)/shard_map/while/body/eval_jaxpr/ppermute | solution.py:29
  158.2 6.9 %collective-permute-start = (f32[192,128]{0,1:T(8,128)S(1)}, f32[192,128]{0,1:T(8,128)S(1)}, u32[]{:S(2)}, u32[]{:S(2)}) collective-permute-start(f32[192,128]{0,1:T(8,128)S(1)} %get-tuple-element.83), channel_id=1, source_target_pairs={{1,0},{2,1},{3,2},{4,3},{5,4},{6,5},{7,6},{8,7},{9,8},{10,9},{11,1... | collective-permute-start | bytes 294920 | tf_op jit(solution)/shard_map/while/body/eval_jaxpr/ppermute | solution.py:19
  160.2 10.2 %collective-permute-start.1 = (f32[192,128]{0,1:T(8,128)S(1)}, f32[192,128]{0,1:T(8,128)S(1)}, u32[]{:S(2)}, u32[]{:S(2)}) collective-permute-start(f32[192,128]{0,1:T(8,128)S(1)} %get-tuple-element.84), channel_id=1, source_target_pairs={{0,1},{1,2},{2,3},{3,4},{4,5},{5,6},{6,7},{7,8},{8,9},{9,10},{10,1... | collective-permute-start | bytes 294920 | tf_op jit(solution)/shard_map/while/body/eval_jaxpr/ppermute | solution.py:17
  173.5 7.2 %collective-permute-start.2 = (f32[384,128]{0,1:T(8,128)}, f32[384,128]{0,1:T(8,128)S(1)}, u32[]{:S(2)}, u32[]{:S(2)}) collective-permute-start(f32[384,128]{0,1:T(8,128)} %fusion.42), channel_id=1, source_target_pairs={{0,64},{64,128},{128,192},{192,256},{256,320},{320,384},{384,448},... | collective-permute-start | bytes 589832 | tf_op jit(solution)/shard_map/while/body/eval_jaxpr/ppermute | solution.py:29
  180.8 6.9 %collective-permute-start = (f32[192,128]{0,1:T(8,128)S(1)}, f32[192,128]{0,1:T(8,128)S(1)}, u32[]{:S(2)}, u32[]{:S(2)}) collective-permute-start(f32[192,128]{0,1:T(8,128)S(1)} %get-tuple-element.83), channel_id=1, source_target_pairs={{1,0},{2,1},{3,2},{4,3},{5,4},{6,5},{7,6},{8,7},{9,8},{10,9},{11,1... | collective-permute-start | bytes 294920 | tf_op jit(solution)/shard_map/while/body/eval_jaxpr/ppermute | solution.py:19
  182.7 10.2 %collective-permute-start.1 = (f32[192,128]{0,1:T(8,128)S(1)}, f32[192,128]{0,1:T(8,128)S(1)}, u32[]{:S(2)}, u32[]{:S(2)}) collective-permute-start(f32[192,128]{0,1:T(8,128)S(1)} %get-tuple-element.84), channel_id=1, source_target_pairs={{0,1},{1,2},{2,3},{3,4},{4,5},{5,6},{6,7},{7,8},{8,9},{9,10},{10,1... | collective-permute-start | bytes 294920 | tf_op jit(solution)/shard_map/while/body/eval_jaxpr/ppermute | solution.py:17
  196.1 7.2 %collective-permute-start.2 = (f32[384,128]{0,1:T(8,128)}, f32[384,128]{0,1:T(8,128)S(1)}, u32[]{:S(2)}, u32[]{:S(2)}) collective-permute-start(f32[384,128]{0,1:T(8,128)} %fusion.42), channel_id=1, source_target_pairs={{0,64},{64,128},{128,192},{192,256},{256,320},{320,384},{384,448},... | collective-permute-start | bytes 589832 | tf_op jit(solution)/shard_map/while/body/eval_jaxpr/ppermute | solution.py:29
  203.4 6.9 %collective-permute-start = (f32[192,128]{0,1:T(8,128)S(1)}, f32[192,128]{0,1:T(8,128)S(1)}, u32[]{:S(2)}, u32[]{:S(2)}) collective-permute-start(f32[192,128]{0,1:T(8,128)S(1)} %get-tuple-element.83), channel_id=1, source_target_pairs={{1,0},{2,1},{3,2},{4,3},{5,4},{6,5},{7,6},{8,7},{9,8},{10,9},{11,1... | collective-permute-start | bytes 294920 | tf_op jit(solution)/shard_map/while/body/eval_jaxpr/ppermute | solution.py:19
  205.3 10.2 %collective-permute-start.1 = (f32[192,128]{0,1:T(8,128)S(1)}, f32[192,128]{0,1:T(8,128)S(1)}, u32[]{:S(2)}, u32[]{:S(2)}) collective-permute-start(f32[192,128]{0,1:T(8,128)S(1)} %get-tuple-element.84), channel_id=1, source_target_pairs={{0,1},{1,2},{2,3},{3,4},{4,5},{5,6},{6,7},{7,8},{8,9},{9,10},{10,1... | collective-permute-start | bytes 294920 | tf_op jit(solution)/shard_map/while/body/eval_jaxpr/ppermute | solution.py:17
  218.7 7.2 %collective-permute-start.2 = (f32[384,128]{0,1:T(8,128)}, f32[384,128]{0,1:T(8,128)S(1)}, u32[]{:S(2)}, u32[]{:S(2)}) collective-permute-start(f32[384,128]{0,1:T(8,128)} %fusion.42), channel_id=1, source_target_pairs={{0,64},{64,128},{128,192},{192,256},{256,320},{320,384},{384,448},... | collective-permute-start | bytes 589832 | tf_op jit(solution)/shard_map/while/body/eval_jaxpr/ppermute | solution.py:29
  226.0 10.2 %collective-permute-start.8 = (f32[192,128]{0,1:T(8,128)S(1)}, f32[192,128]{0,1:T(8,128)S(1)}, u32[]{:S(2)}, u32[]{:S(2)}) collective-permute-start(f32[192,128]{0,1:T(8,128)S(1)} %get-tuple-element.54), channel_id=1, source_target_pairs={{0,1},{1,2},{2,3},{3,4},{4,5},{5,6},{6,7},{7,8},{8,9},{9,10},{10,1... | collective-permute-start | bytes 294920 | tf_op jit(solution)/shard_map/ppermute | solution.py:17
  227.9 9.7 %collective-permute-start.9 = (f32[192,128]{0,1:T(8,128)S(1)}, f32[192,128]{0,1:T(8,128)S(1)}, u32[]{:S(2)}, u32[]{:S(2)}) collective-permute-start(f32[192,128]{0,1:T(8,128)S(1)} %get-tuple-element.55), channel_id=1, source_target_pairs={{1,0},{2,1},{3,2},{4,3},{5,4},{6,5},{7,6},{8,7},{9,8},{10,9},{11,1... | collective-permute-start | bytes 294920 | tf_op jit(solution)/shard_map/ppermute | solution.py:19
where the time goes:
time: 245 us; the launch traced here: 243 us
  starting transfers between devices  94.2 us (38%)
  waiting for transfers between devices  88.6 us (36%)
  matrix products  42.6 us (17%)
  local copies, waits for them, and re-layouts  12.2 us (5%)
  other arithmetic  5.16 us (2%)
    ppermute x10, starting transfers between devices, extended_2(): lax.ppermute(head, axis, [((i + 1) % count, i) for i in range(count)])  45.8 us
    ppermute x10, waiting for transfers between devices, extended_2(): lax.ppermute(tail, axis, [(i, (i + 1) % count) for i in range(count)])  41.4 us
    ppermute x8, waiting for transfers between devices, passed_along(): return lax.ppermute(block, axis, route)  36.9 us
    ppermute x10, starting transfers between devices, extended_2(): lax.ppermute(tail, axis, [(i, (i + 1) % count) for i in range(count)])  33.1 us
    dot_general x8, matrix products, coarse_apply(): return jnp.dot(coarse_op, extended, precision=lax.Precision.HIGHEST)  24.7 us
    ppermute x8, starting transfers between devices, passed_along(): return lax.ppermute(block, axis, route)  15.3 us
    dot_general x2, matrix products, on_device(): jnp.einsum('bkij,bkjn->bin', transport, pieces, precision=lax.Precision.H...  11.3 us
    ppermute x10, waiting for transfers between devices, extended_2(): lax.ppermute(head, axis, [((i + 1) % count, i) for i in range(count)])  10.3 us
  transfers between devices with their start and end apart: 28, of which 25 were waited for; matrix products, arithmetic and copies ran while one was open for 10% of the time, Pallas kernels for 0%

commit v1 on v0

v1 whole, which is shorter than its diff:
```python
import jax
import jax.numpy as jnp
from jax import lax
from jax.experimental import pallas as pl
from jax.experimental.pallas import tpu as pltpu
from jax.sharding import PartitionSpec as P

HALO = 256
BS = 128
F32 = jnp.float32
BF16 = jnp.bfloat16
VMEM = pl.BlockSpec(memory_space=pltpu.VMEM)
SMEM = pl.BlockSpec(memory_space=pltpu.SMEM)


def call(kernel, outs, in_specs, flops, nbytes, scratch=()):
    return pl.pallas_call(
        kernel,
        out_shape=[jax.ShapeDtypeStruct(shape, dtype) for shape, dtype in outs],
        in_specs=in_specs,
        out_specs=[VMEM] * len(outs),
        scratch_shapes=list(scratch),
        cost_estimate=pl.CostEstimate(flops=flops, bytes_accessed=nbytes, transcendentals=0),
        compiler_params=pltpu.CompilerParams(vmem_limit_bytes=40 << 20),
    )


def halves(value):
    high = value.astype(BF16)
    return high, (value - high.astype(F32)).astype(BF16)


def pair(value):
    return jnp.concatenate(halves(value), axis=1)


def dot(a, b):
    return jnp.dot(a, b, preferred_element_type=F32)


def folded(product):
    width = product.shape[1] // 2
    return product[:, :width] + product[:, width:]


def prepare(live_ref, ops_ref, map_ref, starts_ref, coarse_ref,
            high_ref, low_ref, gather_ref, spread_ref, inverse_ref, own_ref, rstart_ref, coarse2_ref):
    blocks, slots = ops_ref.shape[:2]
    coarse = coarse_ref.shape[0]
    for b in range(blocks):
        for k in range(slots):
            high, low = halves(jnp.where(k < live_ref[b], ops_ref[b, k], 0.0))
            high_ref[b, :, k * BS:(k + 1) * BS] = high
            low_ref[b, :, k * BS:(k + 1) * BS] = low
        own_ref[b * BS:(b + 1) * BS, :] = pair(starts_ref[b * BS:(b + 1) * BS, :])
    cells = lax.broadcasted_iota(jnp.int32, (coarse, BS), 0)
    children = jnp.zeros((coarse, 1), F32)
    for b in range(blocks):
        chosen = jnp.where(map_ref[b:b + 1, :] == cells, 1.0, 0.0)
        children = children + jnp.sum(chosen, axis=1, keepdims=True)
        gather_ref[:, b * BS:(b + 1) * BS] = chosen.astype(BF16)
        spread_ref[b * BS:(b + 1) * BS, :] = chosen.T.astype(BF16)
    inverse = jnp.broadcast_to(1.0 / children, inverse_ref.shape)
    inverse_ref[...] = inverse
    rstart_ref[...] = folded(dot(gather_ref[...], own_ref[...])) * inverse
    width = coarse_ref.shape[1]
    high, low = halves(coarse_ref[...])
    coarse2_ref[:, :width] = high
    coarse2_ref[:, width:] = low


def transport(cols_ref, high_ref, low_ref, own_ref, before_ref, after_ref, sources_ref, window, emit):
    rows = own_ref.shape[0]
    blocks = high_ref.shape[0]
    slots = high_ref.shape[2] // BS
    window[0:HALO, :] = pair(before_ref[...])
    window[HALO:HALO + rows, :] = own_ref[...]
    window[HALO + rows:, :] = pair(after_ref[...])
    for b in range(blocks):
        pieces = []
        for k in range(slots):
            at = pl.multiple_of(cols_ref[b * slots + k] * BS, BS)
            pieces.append(window[pl.ds(at, BS), :])
        pieces = jnp.concatenate(pieces, axis=0)
        tracers = pieces.shape[1] // 2
        value = folded(dot(high_ref[b], pieces)) + dot(low_ref[b], pieces[:, :tracers])
        emit(b, value + sources_ref[b * BS:(b + 1) * BS, :])


def first_step(cols_ref, high_ref, low_ref, own_ref, before_ref, after_ref, sources_ref,
               next_ref, head_ref, tail_ref, window):
    blocks = high_ref.shape[0]
    ends = HALO // BS

    def emit(b, value):
        next_ref[b * BS:(b + 1) * BS, :] = pair(value)
        if b < ends:
            head_ref[b * BS:(b + 1) * BS, :] = value
        if b >= blocks - ends:
            at = b - blocks + ends
            tail_ref[at * BS:(at + 1) * BS, :] = value

    transport(cols_ref, high_ref, low_ref, own_ref, before_ref, after_ref, sources_ref, window, emit)


def second_step(cols_ref, high_ref, low_ref, own_ref, before_ref, after_ref, sources_ref,
                gather_ref, inverse_ref, following_ref,
                end_ref, jump_ref, head_ref, tail_ref, window, split):
    def emit(b, value):
        end_ref[b * BS:(b + 1) * BS, :] = value
        split[b * BS:(b + 1) * BS, :] = pair(value)

    transport(cols_ref, high_ref, low_ref, own_ref, before_ref, after_ref, sources_ref, window, emit)
    jump = folded(dot(gather_ref[...], split[...])) * inverse_ref[...] - following_ref[...]
    rim = head_ref.shape[0]
    jump_ref[...] = jump
    head_ref[...] = jump[:rim]
    tail_ref[...] = jump[jump.shape[0] - rim:]


def coarse_product(coarse2_ref, before_ref, own_ref, after_ref):
    width = coarse2_ref.shape[1] // 2
    extended = jnp.concatenate([pair(before_ref[...]), pair(own_ref[...]), pair(after_ref[...])], axis=0)
    tracers = extended.shape[1] // 2
    return folded(dot(coarse2_ref[:, :width], extended)) + dot(coarse2_ref[:, width:], extended[:, :tracers])


def advance(coarse2_ref, before_ref, own_ref, after_ref, jump_ref, image_ref,
            state_ref, head_ref, tail_ref, total_ref):
    image = coarse_product(coarse2_ref, before_ref, own_ref, after_ref)
    state = image + jump_ref[...]
    rim = head_ref.shape[0]
    head_ref[...] = state[:rim]
    tail_ref[...] = state[state.shape[0] - rim:]
    state_ref[...] = state
    total_ref[...] = image_ref[...] + image


def finish(coarse2_ref, before_ref, own_ref, after_ref, image_ref, spread_ref, end_ref, out_ref):
    image = image_ref[...] + coarse_product(coarse2_ref, before_ref, own_ref, after_ref)
    split = pair(image)
    for b in range(end_ref.shape[0] // BS):
        rows = slice(b * BS, (b + 1) * BS)
        out_ref[rows, :] = end_ref[rows, :] + folded(dot(spread_ref[rows, :], split))


def ring_pair(head, tail, axis):
    count = lax.axis_size(axis)
    before = lax.ppermute(tail, axis, [(i, (i + 1) % count) for i in range(count)])
    after = lax.ppermute(head, axis, [((i + 1) % count, i) for i in range(count)])
    return before, after


def on_device(starts, sources, fine_ops, col_index, live_count, coarse_op, cell_map):
    first_state = starts[0]
    transport_ops = fine_ops[0]
    rows, tracers = first_state.shape
    blocks, slots = transport_ops.shape[:2]
    columns = col_index[0].reshape(-1)
    live = live_count[0]
    coarse, reach = coarse_op.shape
    rim = (reach - coarse) // 2
    slices = lax.axis_size("tm")
    tiles = lax.axis_size("tile")
    window = rows + 2 * HALO
    step_flops = 6 * rows * slots * BS * tracers
    coarse_flops = 6 * coarse * reach * tracers

    before, after = ring_pair(first_state[:HALO], first_state[rows - HALO:], "tile")
    high, low, gather, spread, inverse, own, rstart, coarse2 = call(
        prepare,
        [((blocks, BS, slots * BS), BF16), ((blocks, BS, slots * BS), BF16), ((coarse, rows), BF16),
         ((rows, coarse), BF16), ((coarse, tracers), F32), ((rows, 2 * tracers), BF16),
         ((coarse, tracers), F32), ((coarse, 2 * reach), BF16)],
        [SMEM, VMEM, VMEM, VMEM, VMEM], 4 * coarse * rows * tracers, 14_000_000,
    )(live, transport_ops, cell_map.reshape(-1, BS), first_state, coarse_op)
    following = lax.ppermute(rstart, "tm", [(i + 1, i) for i in range(slices - 1)])

    step_in = [SMEM] + [VMEM] * 6
    state, head, tail = call(
        first_step,
        [((rows, 2 * tracers), BF16), ((HALO, tracers), F32), ((HALO, tracers), F32)],
        step_in, step_flops, 6_000_000, [pltpu.VMEM((window, 2 * tracers), BF16)],
    )(columns, high, low, own, before, after, sources)
    before, after = ring_pair(head, tail, "tile")
    fine_end, jump, head, tail = call(
        second_step,
        [((rows, tracers), F32), ((coarse, tracers), F32), ((rim, tracers), F32), ((rim, tracers), F32)],
        step_in + [VMEM] * 3, step_flops + 4 * coarse * rows * tracers, 8_000_000,
        [pltpu.VMEM((window, 2 * tracers), BF16), pltpu.VMEM((rows, 2 * tracers), BF16)],
    )(columns, high, low, state, before, after, sources, gather, inverse, following)

    def to_slice(block, n, shift):
        route = [((n - 1) * tiles + i, n * tiles + (i + shift) % tiles) for i in range(tiles)]
        return lax.ppermute(block, ("tm", "tile"), route)

    image = jnp.zeros((coarse, tracers), F32)
    state = jump
    for n in range(1, slices):
        before = to_slice(tail, n, 1)
        after = to_slice(head, n, -1)
        own = to_slice(state, n, 0)
        if n < slices - 1:
            state, head, tail, image = call(
                advance,
                [((coarse, tracers), F32), ((rim, tracers), F32), ((rim, tracers), F32), ((coarse, tracers), F32)],
                [VMEM] * 6, coarse_flops, 2_000_000,
            )(coarse2, before, own, after, jump, image)
        else:
            (result,) = call(
                finish, [((rows, tracers), F32)], [VMEM] * 7,
                coarse_flops + 4 * coarse * rows * tracers, 4_000_000,
            )(coarse2, before, own, after, image, spread, fine_end)
    return result[None]


def solution(mesh):
    placed = (
        P("tm", "tile", None),
        P("tile", None),
        P("tm", "tile", None, None, None),
        P("tm", "tile", None),
        P("tm", "tile"),
        P("tile", None),
        P("tile"),
    )
    return jax.shard_map(
        on_device, mesh=mesh, in_specs=placed, out_specs=P("tm", "tile", None), check_vma=False
    )
```

time: 245 us -> 120 us (0.49)
  starting transfers between devices: 94.2 us -> 44.8 us
  matrix products: 42.6 us -> 0 us
  waiting for transfers between devices: 88.6 us -> 47.1 us
  Pallas kernels: 0 us -> 11.9 us
  other arithmetic: 5.16 us -> 0 us
  local copies, waits for them, and re-layouts: 12.2 us -> 14.9 us
    ppermute x28 -> x26, starting transfers between devices: 94.2 us -> 44.8 us  [the longest x2 19.2 us: ring_pair(): lax.ppermute(head, axis, [((i + 1) % count, i) for i in range(count)])]
    dot_general x12 -> x0, matrix products: 42.6 us -> none  [the longest x8 24.7 us: coarse_apply(): return jnp.dot(coarse_op, extended, precision=lax.Precision.HIGHEST)]
    ppermute x28 -> x26, waiting for transfers between devices: 88.6 us -> 47.1 us  [the longest x21 43.3 us: to_slice(): return lax.ppermute(block, ('tm', 'tile'), route)]
    unnamed x12 -> x35, local copies, waits for them, and re-layouts: 0.89 us -> 13.1 us
    pallas_call x0 -> x10, Pallas kernels: none -> 11.9 us  [the longest x6 2.88 us: on_device(): call(advance, [((coarse, tracers), F32), ((rim, tracers), F32), ((rim, tr...]
    gather x2 -> x0, local copies, waits for them, and re-layouts: 7.23 us -> none  [on_device(): fine_extended.reshape(-1, block_size, tracers)[columns]]
    concatenate x2 -> x0, other arithmetic: 3.27 us -> none  [extended_2(): jnp.concatenate([lax.ppermute(tail, axis, [(i, (i + 1) % count) for i in...]
  transfers between devices with their start and end apart: 28 -> 26, of which waited for: 25 -> 5; matrix products, arithmetic and copies ran while one was open for 10% -> 0% of each run, Pallas kernels for 0% -> 4%
where the time goes in v1:
time: 120 us; the launch traced here: 119 us
  waiting for transfers between devices  47.1 us (39%)
  starting transfers between devices  44.8 us (37%)
  local copies, waits for them, and re-layouts  14.9 us (12%)
  Pallas kernels  11.9 us (10%)
    ppermute x21, waiting for transfers between devices, to_slice(): return lax.ppermute(block, ('tm', 'tile'), route)  43.3 us
    ppermute x2, starting transfers between devices, ring_pair(): lax.ppermute(head, axis, [((i + 1) % count, i) for i in range(count)])  19.2 us
    ppermute x21, starting transfers between devices, to_slice(): return lax.ppermute(block, ('tm', 'tile'), route)  17.9 us
    unnamed x35, local copies, waits for them, and re-layouts  13.1 us
    ppermute x2, starting transfers between devices, ring_pair(): lax.ppermute(tail, axis, [(i, (i + 1) % count) for i in range(count)])  5.74 us
    pallas_call x6, Pallas kernels, on_device(): call(advance, [((coarse, tracers), F32), ((rim, tracers), F32), ((rim, tr...  2.88 us
    pallas_call x1, Pallas kernels, on_device(): call(prepare, [((blocks, BS, slots * BS), BF16), ((blocks, BS, slots * BS...  2.71 us
  transfers between devices with their start and end apart: 26, of which 5 were waited for; matrix products, arithmetic and copies ran while one was open for 0% of the time, Pallas kernels for 4%

profile of v1, /device:TPU:6, one launch (start us, length us, event | category | flops | bytes accessed | tf_op | source)
XLA Modules:
  0.0 119.1 jit_solution(5029744532787379144)
XLA Ops:
  0.0 1.7 %slice_bitcast_fusion = (f32[256,128]{1,0:T(8,128)}, f32[256,128]{1,0:T(8,128)}) fusion(f32[1,1536,128]{2,1,0:T(8,128)} %param.7), kind=kLoop, calls=%fused_computation | loop fusion | bytes 524288 | tf_op jit(solution)/shard_map/slice | solution.py:169
  1.7 3.8 %collective-permute-start = (f32[256,128]{1,0:T(8,128)}, f32[256,128]{1,0:T(8,128)}, u32[]{:S(2)}, u32[]{:S(2)}) collective-permute-start(f32[256,128]{1,0:T(8,128)} %get-tuple-element.84), channel_id=1, source_target_pairs={{0,1},{1,2},{2,3},{3,4},{4,5},{5,6},{6,7},{7,8},{8,9},{9,10},{10,1... | collective-permute-start | bytes 393224 | tf_op jit(solution)/shard_map/ppermute | solution.py:149
  5.5 11.9 %collective-permute-start.1 = (f32[256,128]{1,0:T(8,128)}, f32[256,128]{1,0:T(8,128)}, u32[]{:S(2)}, u32[]{:S(2)}) collective-permute-start(f32[256,128]{1,0:T(8,128)} %get-tuple-element.83), channel_id=1, source_target_pairs={{1,0},{2,1},{3,2},{4,3},{5,4},{6,5},{7,6},{8,7},{9,8},{10,9},{11,1... | collective-permute-start | bytes 393224 | tf_op jit(solution)/shard_map/ppermute | solution.py:150
  17.5 1.9 %copy-done.2 = f32[1,12,4,128,128]{4,3,2,1,0:T(8,128)S(1)} copy-done((f32[1,12,4,128,128]{4,3,2,1,0:T(8,128)S(1)}, f32[1,12,4,128,128]{4,3,2,1,0:T(8,128)}, u32[]{:S(2)}) %copy-start.2) | copy-done | bytes 3145752
  19.4 1.1 copy-done.4
  20.5 1.3 %copy-done.5 = f32[384,768]{1,0:T(8,128)S(1)} copy-done((f32[384,768]{1,0:T(8,128)S(1)}, f32[384,768]{1,0:T(8,128)}, u32[]{:S(2)}) %copy-start.5) | copy-done | bytes 1179672
  21.8 0.7 copy-done.14
  22.5 0.7 copy-done.15
  23.1 2.7 %shard_map.73 = (bf16[12,128,512]{2,1,0:T(8,128)(2,1)S(1)}, bf16[12,128,512]{2,1,0:T(8,128)(2,1)S(1)}, bf16[384,1536]{1,0:T(8,128)(2,1)S(1)}, bf16[1536,384]{1,0...) custom-call(s32[12]{0:T(128)S(1)} %bitcast.12, ...), custom_call_target="tpu_custom_call" | custom-call | flops 301989888 | bytes 14000000 | tf_op jit(solution)/shard_map/pallas_call | solution.py:170
  25.8 1.2 copy-done
  27.0 1.0 copy-done.6
  28.0 1.0 copy-done.8
  29.1 0.9 copy-done.10
  29.9 0.7 copy-done.12
  30.6 1.9 %collective-permute-start.4 = (f32[384,128]{1,0:T(8,128)}, f32[384,128]{1,0:T(8,128)}, u32[]{:S(2)}, u32[]{:S(2)}) collective-permute-start(f32[384,128]{1,0:T(8,128)} %get-tuple-element.53), channel_id=1, source_target_pairs={{64,0},{128,64},{192,128},{256,192},{320,256},{384,320},{448,384},... | collective-permute-start | bytes 589832 | tf_op jit(solution)/shard_map/ppermute | solution.py:177
  32.8 1.4 %copy-done.1 = bf16[12,128,512]{2,1,0:T(8,128)(2,1)S(1)} copy-done((bf16[12,128,512]{2,1,0:T(8,128)(2,1)S(1)}, bf16[12,128,512]{2,1,0:T(8,128)(2,1)}, u32[]{:S(2)}) %copy-start.1) | copy-done | bytes 1572888
  34.2 1.1 copy-done.11
  35.3 2.2 %shard_map.74 = (bf16[1536,256]{1,0:T(8,128)(2,1)S(1)}, f32[256,128]{1,0:T(8,128)S(1)}, f32[256,128]{1,0:T(8,128)S(1)}) custom-call(s32[48]{0:T(128)S(1)} %reshape_squeeze.3.cols_ref, bf16[12,128,512]{2,1,0:T(8,128)(2,1)S(1)} %get-tuple-element.45.high_ref, bf16[12,128,512]{2,1,0:T(8,128)(2,1)S(1)} %copy-done.1, bf16[1536,256]{1,0:T(8,128)(2,1)S(1)} %copy-done.11, ...), custom_call_target="tpu_custom_call" | custom-call | flops 603979776 | bytes 6000000 | tf_op jit(solution)/shard_map/pallas_call | solution.py:180
  37.5 1.9 %collective-permute-start.2 = (f32[256,128]{1,0:T(8,128)S(1)}, f32[256,128]{1,0:T(8,128)S(1)}, u32[]{:S(2)}, u32[]{:S(2)}) collective-permute-start(f32[256,128]{1,0:T(8,128)S(1)} %get-tuple-element.49), channel_id=1, source_target_pairs={{0,1},{1,2},{2,3},{3,4},{4,5},{5,6},{6,7},{7,8},{8,9},{9,10},{10,1... | collective-permute-start | bytes 393224 | tf_op jit(solution)/shard_map/ppermute | solution.py:149
  39.4 7.2 %collective-permute-start.3 = (f32[256,128]{1,0:T(8,128)S(1)}, f32[256,128]{1,0:T(8,128)S(1)}, u32[]{:S(2)}, u32[]{:S(2)}) collective-permute-start(f32[256,128]{1,0:T(8,128)S(1)} %get-tuple-element.50), channel_id=1, source_target_pairs={{1,0},{2,1},{3,2},{4,3},{5,4},{6,5},{7,6},{8,7},{9,8},{10,9},{11,1... | collective-permute-start | bytes 393224 | tf_op jit(solution)/shard_map/ppermute | solution.py:150
  46.7 2.2 %collective-permute-done.2.before_ref = f32[256,128]{1,0:T(8,128)S(1)} collective-permute-done((f32[256,128]{1,0:T(8,128)S(1)}, f32[256,128]{1,0:T(8,128)S(1)}, u32[]{:S(2)}, u32[]{:S(2)}) %collective-permute-start.2) | collective-permute-done | bytes 131104 | tf_op jit(solution)/shard_map/ppermute | solution.py:149
  48.9 1.6 %collective-permute-done.3.after_ref = f32[256,128]{1,0:T(8,128)S(1)} collective-permute-done((f32[256,128]{1,0:T(8,128)S(1)}, f32[256,128]{1,0:T(8,128)S(1)}, u32[]{:S(2)}, u32[]{:S(2)}) %collective-permute-start.3) | collective-permute-done | bytes 131104 | tf_op jit(solution)/shard_map/ppermute | solution.py:150
  50.4 2.3 %shard_map.75 = (f32[1536,128]{1,0:T(8,128)S(1)}, f32[384,128]{1,0:T(8,128)S(1)}, f32[192,128]{1,0:T(8,128)S(1)}, f32[192,128]{1,0:T(8,128)S(1)}) custom-call(s32[48]{0:T(128)S(1)} %reshape_squeeze.3.cols_ref, bf16[12,128,512]{2,1,0:T(8,128)(2,1)S(1)} %get-tuple-element.45.high_ref, bf16[12,128,512]{2,1,0:T(8,128)(2,1)S(1)} %copy-done.1, ...), custom_call_target="tpu_custom_call" | custom-call | flops 905969664 | bytes 8000000 | tf_op jit(solution)/shard_map/pallas_call | solution.py:186
  52.8 0.7 collective-permute-start.6
  53.4 0.7 collective-permute-start.5
  54.1 0.7 collective-permute-start.7
  55.3 0.7 collective-permute-start.9
  56.0 0.7 collective-permute-start.10
  56.7 0.7 collective-permute-start.8
  57.9 0.7 collective-permute-start.12
  58.6 0.7 collective-permute-start.11
  59.2 0.7 collective-permute-start.13
  60.4 0.7 collective-permute-start.15
  61.1 0.7 collective-permute-start.14
  61.8 0.7 collective-permute-start.16
  63.0 0.7 collective-permute-start.18
  63.7 0.7 collective-permute-start.17
  64.3 0.7 collective-permute-start.19
  65.5 1.4 %collective-permute-start.21 = (f32[384,128]{1,0:T(8,128)S(1)}, f32[384,128]{1,0:T(8,128)S(1)}, u32[]{:S(2)}, u32[]{:S(2)}) collective-permute-start(f32[384,128]{1,0:T(8,128)S(1)} %get-tuple-element.74), channel_id=1, source_target_pairs={{320,384},{321,385},{322,386},{323,387},{324,388},{325,389},{326,3... | collective-permute-start | bytes 589832 | tf_op jit(solution)/shard_map/ppermute | solution.py:195
  67.0 1.3 %collective-permute-start.20 = (f32[192,128]{1,0:T(8,128)S(1)}, f32[192,128]{1,0:T(8,128)S(1)}, u32[]{:S(2)}, u32[]{:S(2)}) collective-permute-start(f32[192,128]{1,0:T(8,128)S(1)} %get-tuple-element.73), channel_id=1, source_target_pairs={{320,385},{321,386},{322,387},{323,388},{324,389},{325,390},{326,3... | collective-permute-start | bytes 294920 | tf_op jit(solution)/shard_map/ppermute | solution.py:195
  68.3 1.3 %collective-permute-start.22 = (f32[192,128]{1,0:T(8,128)S(1)}, f32[192,128]{1,0:T(8,128)S(1)}, u32[]{:S(2)}, u32[]{:S(2)}) collective-permute-start(f32[192,128]{1,0:T(8,128)S(1)} %get-tuple-element.75), channel_id=1, source_target_pairs={{320,447},{321,384},{322,385},{323,386},{324,387},{325,388},{326,3... | collective-permute-start | bytes 294920 | tf_op jit(solution)/shard_map/ppermute | solution.py:195
  69.6 41.1 %collective-permute-done.20.before_ref = f32[192,128]{1,0:T(8,128)S(1)} collective-permute-done((f32[192,128]{1,0:T(8,128)S(1)}, f32[192,128]{1,0:T(8,128)S(1)}, u32[]{:S(2)}, u32[]{:S(2)}) %collective-permute-start.20) | collective-permute-done | bytes 98336 | tf_op jit(solution)/shard_map/ppermute | solution.py:195
  111.1 1.3 %collective-permute-start.24 = (f32[384,128]{1,0:T(8,128)S(1)}, f32[384,128]{1,0:T(8,128)S(1)}, u32[]{:S(2)}, u32[]{:S(2)}) collective-permute-start(f32[384,128]{1,0:T(8,128)S(1)} %get-tuple-element.78), channel_id=1, source_target_pairs={{384,448},{385,449},{386,450},{387,451},{388,452},{389,453},{390,4... | collective-permute-start | bytes 589832 | tf_op jit(solution)/shard_map/ppermute | solution.py:195
  112.4 1.3 %collective-permute-start.23 = (f32[192,128]{1,0:T(8,128)S(1)}, f32[192,128]{1,0:T(8,128)S(1)}, u32[]{:S(2)}, u32[]{:S(2)}) collective-permute-start(f32[192,128]{1,0:T(8,128)S(1)} %get-tuple-element.77), channel_id=1, source_target_pairs={{384,449},{385,450},{386,451},{387,452},{388,453},{389,454},{390,4... | collective-permute-start | bytes 294920 | tf_op jit(solution)/shard_map/ppermute | solution.py:195
  113.7 1.3 %collective-permute-start.25 = (f32[192,128]{1,0:T(8,128)S(1)}, f32[192,128]{1,0:T(8,128)S(1)}, u32[]{:S(2)}, u32[]{:S(2)}) collective-permute-start(f32[192,128]{1,0:T(8,128)S(1)} %get-tuple-element.79), channel_id=1, source_target_pairs={{384,511},{385,448},{386,449},{387,450},{388,451},{389,452},{390,4... | collective-permute-start | bytes 294920 | tf_op jit(solution)/shard_map/ppermute | solution.py:195
  115.0 0.9 collective-permute-done.23.before_ref
  115.9 1.3 %collective-permute-done.25.after_ref = f32[192,128]{1,0:T(8,128)S(1)} collective-permute-done((f32[192,128]{1,0:T(8,128)S(1)}, f32[192,128]{1,0:T(8,128)S(1)}, u32[]{:S(2)}, u32[]{:S(2)}) %collective-permute-start.25) | collective-permute-done | bytes 98336 | tf_op jit(solution)/shard_map/ppermute | solution.py:195
  117.2 1.9 %shard_map.82 = f32[1536,128]{1,0:T(8,128)} custom-call(bf16[384,1536]{1,0:T(8,128)(2,1)S(1)} %get-tuple-element.44.coarse2_ref, f32[192,128]{1,0:T(8,128)S(1)} %collective-permute-done.23.before_ref, f32[384,128]{1,0:T(8,128)S(1)} %collective-permute-done.24.own_ref, f32[192,128]{1,0:T(8,128)S(1)} %collective-permute-done.25.after_ref, ...), custom_call_target="tpu_custom_call" | custom-call | flops 528482304 | bytes 4000000 | tf_op jit(solution)/shard_map/pallas_call | solution.py:210
  (52 shorter events, 3.2 us)
Async XLA Ops:
  1.7 31.0 %collective-permute-start = (f32[256,128]{1,0:T(8,128)}, f32[256,128]{1,0:T(8,128)}, u32[]{:S(2)}, u32[]{:S(2)}) collective-permute-start(f32[256,128]{1,0:T(8,128)} %get-tuple-element.84), channel_id=1, source_target_pairs={{0,1},{1,2},{2,3},{3,4},{4,5},{5,6},{6,7},{7,8},{8,9},{9,10},{10,1... | collective-permute-start | bytes 393224 | tf_op jit(solution)/shard_map/ppermute | solution.py:149
  5.5 27.2 %collective-permute-start.1 = (f32[256,128]{1,0:T(8,128)}, f32[256,128]{1,0:T(8,128)}, u32[]{:S(2)}, u32[]{:S(2)}) collective-permute-start(f32[256,128]{1,0:T(8,128)} %get-tuple-element.83), channel_id=1, source_target_pairs={{1,0},{2,1},{3,2},{4,3},{5,4},{6,5},{7,6},{8,7},{9,8},{10,9},{11,1... | collective-permute-start | bytes 393224 | tf_op jit(solution)/shard_map/ppermute | solution.py:150
  17.5 1.9 %copy-start.2 = (f32[1,12,4,128,128]{4,3,2,1,0:T(8,128)S(1)}, f32[1,12,4,128,128]{4,3,2,1,0:T(8,128)}, u32[]{:S(2)}) copy-start(f32[1,12,4,128,128]{4,3,2,1,0:T(8,128)} %param.9) | copy-start | bytes 9437188
  19.4 1.1 copy-start.4
  20.5 1.3 %copy-start.5 = (f32[384,768]{1,0:T(8,128)S(1)}, f32[384,768]{1,0:T(8,128)}, u32[]{:S(2)}) copy-start(f32[384,768]{1,0:T(8,128)} %coarse_ref.1) | copy-start | bytes 3538948
  21.8 0.7 copy-start.14
  22.5 0.7 copy-start.15
  23.1 9.4 %copy-start.16 = (s32[1,12,4]{1,2,0:T(4,128)S(1)}, s32[1,12,4]{1,2,0:T(4,128)}, u32[]{:S(2)}) copy-start(s32[1,12,4]{1,2,0:T(4,128)} %param.10) | copy-start | bytes 580
  23.1 9.6 %copy-start.3 = (f32[1536,128]{1,0:T(8,128)S(1)}, f32[1536,128]{1,0:T(8,128)}, u32[]{:S(2)}) copy-start(f32[1536,128]{1,0:T(8,128)} %sources_ref.3) | copy-start | bytes 2359300
  25.8 1.2 copy-start
  27.0 1.0 copy-start.6
  28.0 1.0 copy-start.8
  29.1 0.9 copy-start.10
  29.9 0.7 copy-start.12
  30.6 16.0 %collective-permute-start.4 = (f32[384,128]{1,0:T(8,128)}, f32[384,128]{1,0:T(8,128)}, u32[]{:S(2)}, u32[]{:S(2)}) collective-permute-start(f32[384,128]{1,0:T(8,128)} %get-tuple-element.53), channel_id=1, source_target_pairs={{64,0},{128,64},{192,128},{256,192},{320,256},{384,320},{448,384},... | collective-permute-start | bytes 589832 | tf_op jit(solution)/shard_map/ppermute | solution.py:177
  32.8 1.4 %copy-start.1 = (bf16[12,128,512]{2,1,0:T(8,128)(2,1)S(1)}, bf16[12,128,512]{2,1,0:T(8,128)(2,1)}, u32[]{:S(2)}) copy-start(bf16[12,128,512]{2,1,0:T(8,128)(2,1)} %copy-done) | copy-start | bytes 4718596
  34.2 1.1 copy-start.11
  35.3 15.1 %copy-start.9 = (bf16[384,1536]{1,0:T(8,128)(2,1)S(1)}, bf16[384,1536]{1,0:T(8,128)(2,1)}, u32[]{:S(2)}) copy-start(bf16[384,1536]{1,0:T(8,128)(2,1)} %copy-done.8) | copy-start | bytes 3538948
  35.3 15.1 %copy-start.13 = (f32[384,128]{1,0:T(8,128)S(1)}, f32[384,128]{1,0:T(8,128)}, u32[]{:S(2)}) copy-start(f32[384,128]{1,0:T(8,128)} %copy-done.12) | copy-start | bytes 589828
  37.5 11.4 %collective-permute-start.2 = (f32[256,128]{1,0:T(8,128)S(1)}, f32[256,128]{1,0:T(8,128)S(1)}, u32[]{:S(2)}, u32[]{:S(2)}) collective-permute-start(f32[256,128]{1,0:T(8,128)S(1)} %get-tuple-element.49), channel_id=1, source_target_pairs={{0,1},{1,2},{2,3},{3,4},{4,5},{5,6},{6,7},{7,8},{8,9},{9,10},{10,1... | collective-permute-start | bytes 393224 | tf_op jit(solution)/shard_map/ppermute | solution.py:149
  39.4 11.0 %collective-permute-start.3 = (f32[256,128]{1,0:T(8,128)S(1)}, f32[256,128]{1,0:T(8,128)S(1)}, u32[]{:S(2)}, u32[]{:S(2)}) collective-permute-start(f32[256,128]{1,0:T(8,128)S(1)} %get-tuple-element.50), channel_id=1, source_target_pairs={{1,0},{2,1},{3,2},{4,3},{5,4},{6,5},{7,6},{8,7},{9,8},{10,9},{11,1... | collective-permute-start | bytes 393224 | tf_op jit(solution)/shard_map/ppermute | solution.py:150
  52.8 2.1 %collective-permute-start.6 = (f32[384,128]{1,0:T(8,128)S(1)}, f32[384,128]{1,0:T(8,128)S(1)}, u32[]{:S(2)}, u32[]{:S(2)}) collective-permute-start(f32[384,128]{1,0:T(8,128)S(1)} %get-tuple-element.55.jump_ref), channel_id=1, source_target_pairs={{0,64},{1,65},{2,66},{3,67},{4,68},{5,69},{6,70},{7,71},{8,72},{9,... | collective-permute-start | bytes 589832 | tf_op jit(solution)/shard_map/ppermute | solution.py:195
  53.4 1.4 %collective-permute-start.5 = (f32[192,128]{1,0:T(8,128)S(1)}, f32[192,128]{1,0:T(8,128)S(1)}, u32[]{:S(2)}, u32[]{:S(2)}) collective-permute-start(f32[192,128]{1,0:T(8,128)S(1)} %get-tuple-element.54), channel_id=1, source_target_pairs={{0,65},{1,66},{2,67},{3,68},{4,69},{5,70},{6,71},{7,72},{8,73},{9,... | collective-permute-start | bytes 294920 | tf_op jit(solution)/shard_map/ppermute | solution.py:195
  54.1 0.7 collective-permute-start.7
  55.3 2.1 %collective-permute-start.9 = (f32[384,128]{1,0:T(8,128)S(1)}, f32[384,128]{1,0:T(8,128)S(1)}, u32[]{:S(2)}, u32[]{:S(2)}) collective-permute-start(f32[384,128]{1,0:T(8,128)S(1)} %get-tuple-element.58), channel_id=1, source_target_pairs={{64,128},{65,129},{66,130},{67,131},{68,132},{69,133},{70,134},{71... | collective-permute-start | bytes 589832 | tf_op jit(solution)/shard_map/ppermute | solution.py:195
  56.0 1.4 %collective-permute-start.10 = (f32[192,128]{1,0:T(8,128)S(1)}, f32[192,128]{1,0:T(8,128)S(1)}, u32[]{:S(2)}, u32[]{:S(2)}) collective-permute-start(f32[192,128]{1,0:T(8,128)S(1)} %get-tuple-element.59), channel_id=1, source_target_pairs={{64,191},{65,128},{66,129},{67,130},{68,131},{69,132},{70,133},{71... | collective-permute-start | bytes 294920 | tf_op jit(solution)/shard_map/ppermute | solution.py:195
  56.7 0.7 collective-permute-start.8
  57.9 2.1 %collective-permute-start.12 = (f32[384,128]{1,0:T(8,128)S(1)}, f32[384,128]{1,0:T(8,128)S(1)}, u32[]{:S(2)}, u32[]{:S(2)}) collective-permute-start(f32[384,128]{1,0:T(8,128)S(1)} %get-tuple-element.62), channel_id=1, source_target_pairs={{128,192},{129,193},{130,194},{131,195},{132,196},{133,197},{134,1... | collective-permute-start | bytes 589832 | tf_op jit(solution)/shard_map/ppermute | solution.py:195
  58.6 1.4 %collective-permute-start.11 = (f32[192,128]{1,0:T(8,128)S(1)}, f32[192,128]{1,0:T(8,128)S(1)}, u32[]{:S(2)}, u32[]{:S(2)}) collective-permute-start(f32[192,128]{1,0:T(8,128)S(1)} %get-tuple-element.61), channel_id=1, source_target_pairs={{128,193},{129,194},{130,195},{131,196},{132,197},{133,198},{134,1... | collective-permute-start | bytes 294920 | tf_op jit(solution)/shard_map/ppermute | solution.py:195
  59.2 0.7 collective-permute-start.13
  60.4 2.1 %collective-permute-start.15 = (f32[384,128]{1,0:T(8,128)S(1)}, f32[384,128]{1,0:T(8,128)S(1)}, u32[]{:S(2)}, u32[]{:S(2)}) collective-permute-start(f32[384,128]{1,0:T(8,128)S(1)} %get-tuple-element.66), channel_id=1, source_target_pairs={{192,256},{193,257},{194,258},{195,259},{196,260},{197,261},{198,2... | collective-permute-start | bytes 589832 | tf_op jit(solution)/shard_map/ppermute | solution.py:195
  61.1 1.4 %collective-permute-start.14 = (f32[192,128]{1,0:T(8,128)S(1)}, f32[192,128]{1,0:T(8,128)S(1)}, u32[]{:S(2)}, u32[]{:S(2)}) collective-permute-start(f32[192,128]{1,0:T(8,128)S(1)} %get-tuple-element.65), channel_id=1, source_target_pairs={{192,257},{193,258},{194,259},{195,260},{196,261},{197,262},{198,2... | collective-permute-start | bytes 294920 | tf_op jit(solution)/shard_map/ppermute | solution.py:195
  61.8 0.7 collective-permute-start.16
  63.0 2.1 %collective-permute-start.18 = (f32[384,128]{1,0:T(8,128)S(1)}, f32[384,128]{1,0:T(8,128)S(1)}, u32[]{:S(2)}, u32[]{:S(2)}) collective-permute-start(f32[384,128]{1,0:T(8,128)S(1)} %get-tuple-element.70), channel_id=1, source_target_pairs={{256,320},{257,321},{258,322},{259,323},{260,324},{261,325},{262,3... | collective-permute-start | bytes 589832 | tf_op jit(solution)/shard_map/ppermute | solution.py:195
  63.7 1.4 %collective-permute-start.17 = (f32[192,128]{1,0:T(8,128)S(1)}, f32[192,128]{1,0:T(8,128)S(1)}, u32[]{:S(2)}, u32[]{:S(2)}) collective-permute-start(f32[192,128]{1,0:T(8,128)S(1)} %get-tuple-element.69), channel_id=1, source_target_pairs={{256,321},{257,322},{258,323},{259,324},{260,325},{261,326},{262,3... | collective-permute-start | bytes 294920 | tf_op jit(solution)/shard_map/ppermute | solution.py:195
  64.3 0.7 collective-permute-start.19
  65.5 51.7 %copy-start.7 = (bf16[1536,384]{1,0:T(8,128)(2,1)S(1)}, bf16[1536,384]{1,0:T(8,128)(2,1)}, u32[]{:S(2)}) copy-start(bf16[1536,384]{1,0:T(8,128)(2,1)} %copy-done.6) | copy-start | bytes 3538948
  65.5 45.1 %collective-permute-start.21 = (f32[384,128]{1,0:T(8,128)S(1)}, f32[384,128]{1,0:T(8,128)S(1)}, u32[]{:S(2)}, u32[]{:S(2)}) collective-permute-start(f32[384,128]{1,0:T(8,128)S(1)} %get-tuple-element.74), channel_id=1, source_target_pairs={{320,384},{321,385},{322,386},{323,387},{324,388},{325,389},{326,3... | collective-permute-start | bytes 589832 | tf_op jit(solution)/shard_map/ppermute | solution.py:195
  67.0 43.7 %collective-permute-start.20 = (f32[192,128]{1,0:T(8,128)S(1)}, f32[192,128]{1,0:T(8,128)S(1)}, u32[]{:S(2)}, u32[]{:S(2)}) collective-permute-start(f32[192,128]{1,0:T(8,128)S(1)} %get-tuple-element.73), channel_id=1, source_target_pairs={{320,385},{321,386},{322,387},{323,388},{324,389},{325,390},{326,3... | collective-permute-start | bytes 294920 | tf_op jit(solution)/shard_map/ppermute | solution.py:195
  68.3 42.4 %collective-permute-start.22 = (f32[192,128]{1,0:T(8,128)S(1)}, f32[192,128]{1,0:T(8,128)S(1)}, u32[]{:S(2)}, u32[]{:S(2)}) collective-permute-start(f32[192,128]{1,0:T(8,128)S(1)} %get-tuple-element.75), channel_id=1, source_target_pairs={{320,447},{321,384},{322,385},{323,386},{324,387},{325,388},{326,3... | collective-permute-start | bytes 294920 | tf_op jit(solution)/shard_map/ppermute | solution.py:195
  111.1 6.1 %collective-permute-start.24 = (f32[384,128]{1,0:T(8,128)S(1)}, f32[384,128]{1,0:T(8,128)S(1)}, u32[]{:S(2)}, u32[]{:S(2)}) collective-permute-start(f32[384,128]{1,0:T(8,128)S(1)} %get-tuple-element.78), channel_id=1, source_target_pairs={{384,448},{385,449},{386,450},{387,451},{388,452},{389,453},{390,4... | collective-permute-start | bytes 589832 | tf_op jit(solution)/shard_map/ppermute | solution.py:195
  112.4 3.5 %collective-permute-start.23 = (f32[192,128]{1,0:T(8,128)S(1)}, f32[192,128]{1,0:T(8,128)S(1)}, u32[]{:S(2)}, u32[]{:S(2)}) collective-permute-start(f32[192,128]{1,0:T(8,128)S(1)} %get-tuple-element.77), channel_id=1, source_target_pairs={{384,449},{385,450},{386,451},{387,452},{388,453},{389,454},{390,4... | collective-permute-start | bytes 294920 | tf_op jit(solution)/shard_map/ppermute | solution.py:195
  113.7 3.5 %collective-permute-start.25 = (f32[192,128]{1,0:T(8,128)S(1)}, f32[192,128]{1,0:T(8,128)S(1)}, u32[]{:S(2)}, u32[]{:S(2)}) collective-permute-start(f32[192,128]{1,0:T(8,128)S(1)} %get-tuple-element.79), channel_id=1, source_target_pairs={{384,511},{385,448},{386,449},{387,450},{388,451},{389,452},{390,4... | collective-permute-start | bytes 294920 | tf_op jit(solution)/shard_map/ppermute | solution.py:195

commit v2 on v1

v2 whole, which is shorter than its diff:
```python
import jax
import jax.numpy as jnp
from jax import lax
from jax.experimental import pallas as pl
from jax.experimental.pallas import tpu as pltpu
from jax.sharding import PartitionSpec as P


HALO = 256
BS = 128
F32 = jnp.float32
BF16 = jnp.bfloat16
VMEM = pl.BlockSpec(memory_space=pltpu.VMEM)
SMEM = pl.BlockSpec(memory_space=pltpu.SMEM)
HBM = pl.BlockSpec(memory_space=pltpu.HBM)


def call(kernel, outs, in_specs, flops, nbytes, scratch=()):
    return pl.pallas_call(
        kernel,
        out_shape=[jax.ShapeDtypeStruct(shape, dtype) for shape, dtype in outs],
        in_specs=in_specs,
        out_specs=[VMEM] * len(outs),
        scratch_shapes=list(scratch),
        cost_estimate=pl.CostEstimate(flops=flops, bytes_accessed=nbytes, transcendentals=0),
        compiler_params=pltpu.CompilerParams(vmem_limit_bytes=16 << 20),
    )


def kept(value):
    return pltpu.with_memory_space_constraint(value, pltpu.HBM)


def halves(value):
    high = value.astype(BF16)
    return high, (value - high.astype(F32)).astype(BF16)


def pair(value):
    return jnp.concatenate(halves(value), axis=1)


def dot(a, b):
    return jnp.dot(a, b, preferred_element_type=F32)


def folded(product):
    width = product.shape[1] // 2
    return product[:, :width] + product[:, width:]


def odd_tile():
    return lax.rem(lax.axis_index("tile"), 2)


def ends(starts_ref, far_ref, near_ref, sems):
    last = starts_ref.shape[0] - HALO
    odd = odd_tile()
    copies = [
        pltpu.make_async_copy(
            starts_ref.at[pl.ds(pl.multiple_of(side * last, BS), HALO), :], out_ref, sems.at[index]
        )
        for index, (side, out_ref) in enumerate(((odd, far_ref), (1 - odd, near_ref)))
    ]
    for copy in copies:
        copy.start()
    for copy in copies:
        copy.wait()


def run_copies(copies):
    for copy in copies:
        copy.start()
    return copies


def fetch(ops_ref, starts_ref, sources_ref, ops_out, own_ref, sources_out, held, sems):
    copies = run_copies([
        pltpu.make_async_copy(starts_ref, held, sems.at[0]),
        pltpu.make_async_copy(ops_ref, ops_out, sems.at[1]),
        pltpu.make_async_copy(sources_ref, sources_out, sems.at[2]),
    ])
    copies[0].wait()
    for b in range(held.shape[0] // BS):
        own_ref[b * BS:(b + 1) * BS, :] = pair(held[b * BS:(b + 1) * BS, :])
    for copy in copies[1:]:
        copy.wait()


def prepare(map_hbm, coarse_hbm, own_ref, token_ref,
            gather_ref, spread_ref, inverse_ref, rstart_ref, coarse2_ref, map_ref, coarse_ref, sems):
    copies = run_copies([
        pltpu.make_async_copy(map_hbm, map_ref, sems.at[0]),
        pltpu.make_async_copy(coarse_hbm, coarse_ref, sems.at[1]),
    ])
    copies[0].wait()
    coarse = coarse_ref.shape[0]
    cells = lax.broadcasted_iota(jnp.int32, (coarse, BS), 0)
    children = jnp.zeros((coarse, 1), F32)
    for b in range(map_ref.shape[0]):
        chosen = jnp.where(map_ref[b:b + 1, :] == cells, 1.0, 0.0)
        children = children + jnp.sum(chosen, axis=1, keepdims=True)
        gather_ref[:, b * BS:(b + 1) * BS] = chosen.astype(BF16)
        spread_ref[b * BS:(b + 1) * BS, :] = chosen.T.astype(BF16)
    inverse = jnp.broadcast_to(1.0 / children, inverse_ref.shape)
    inverse_ref[...] = inverse
    rstart_ref[...] = folded(dot(gather_ref[...], own_ref[...])) * inverse
    copies[1].wait()
    width = coarse_ref.shape[1]
    high, low = halves(coarse_ref[...])
    coarse2_ref[:, :width] = high
    coarse2_ref[:, width:] = low


def transport(cols_hbm, live_hbm, ops_ref, own_ref, far_ref, near_ref, sources_ref,
              cols_ref, live_ref, window, sems, emit):
    copies = run_copies([
        pltpu.make_async_copy(cols_hbm, cols_ref, sems.at[0]),
        pltpu.make_async_copy(live_hbm, live_ref, sems.at[1]),
    ])
    rows = own_ref.shape[0]
    blocks, slots = ops_ref.shape[:2]
    odd = odd_tile()
    window[pl.ds(pl.multiple_of(odd * (HALO + rows), BS), HALO), :] = pair(far_ref[...])
    window[pl.ds(pl.multiple_of((1 - odd) * (HALO + rows), BS), HALO), :] = pair(near_ref[...])
    window[HALO:HALO + rows, :] = own_ref[...]
    for copy in copies:
        copy.wait()
    for b in range(blocks):
        pieces, highs, lows = [], [], []
        for k in range(slots):
            at = pl.multiple_of(cols_ref[k, b] * BS, BS)
            pieces.append(window[pl.ds(at, BS), :])
            high, low = halves(jnp.where(k < live_ref[0, b], ops_ref[b, k], 0.0))
            highs.append(high)
            lows.append(low)
        pieces = jnp.concatenate(pieces, axis=0)
        tracers = pieces.shape[1] // 2
        value = folded(dot(jnp.concatenate(highs, axis=1), pieces))
        value = value + dot(jnp.concatenate(lows, axis=1), pieces[:, :tracers])
        emit(b, value + sources_ref[b * BS:(b + 1) * BS, :])


def sides(block, far_ref, near_ref, width):
    odd = odd_tile()
    last = block.shape[0] - width
    far_ref[...] = block[pl.ds(pl.multiple_of(odd * last, 64), width), :]
    near_ref[...] = block[pl.ds(pl.multiple_of((1 - odd) * last, 64), width), :]


def first_step(cols_hbm, live_hbm, ops_ref, own_ref, far_ref, near_ref, sources_ref,
               next_ref, nfar_ref, nnear_ref, token_ref, cols_ref, live_ref, window, sems, rims):
    blocks = ops_ref.shape[0]
    side = HALO // BS

    def emit(b, value):
        next_ref[b * BS:(b + 1) * BS, :] = pair(value)
        if b < side:
            rims[b * BS:(b + 1) * BS, :] = value
        if b >= blocks - side:
            at = b - blocks + 2 * side
            rims[at * BS:(at + 1) * BS, :] = value

    transport(cols_hbm, live_hbm, ops_ref, own_ref, far_ref, near_ref, sources_ref,
              cols_ref, live_ref, window, sems, emit)
    sides(rims, nfar_ref, nnear_ref, HALO)
    token_ref[...] = jnp.zeros_like(token_ref)


def second_step(cols_hbm, live_hbm, ops_ref, own_ref, far_ref, near_ref, sources_ref,
                gather_ref, inverse_ref, following_ref,
                end_ref, jump_ref, nfar_ref, nnear_ref, cols_ref, live_ref, window, sems, split):
    def emit(b, value):
        end_ref[b * BS:(b + 1) * BS, :] = value
        split[b * BS:(b + 1) * BS, :] = pair(value)

    transport(cols_hbm, live_hbm, ops_ref, own_ref, far_ref, near_ref, sources_ref,
              cols_ref, live_ref, window, sems, emit)
    jump_ref[...] = folded(dot(gather_ref[...], split[...])) * inverse_ref[...] - following_ref[...]
    sides(jump_ref, nfar_ref, nnear_ref, nfar_ref.shape[0])


def coarse_product(coarse2_ref, far_ref, own_ref, near_ref, window):
    width = coarse2_ref.shape[1] // 2
    rim, rows = far_ref.shape[0], own_ref.shape[0]
    odd = odd_tile()
    window[pl.ds(pl.multiple_of(odd * (rim + rows), 64), rim), :] = pair(far_ref[...])
    window[pl.ds(pl.multiple_of((1 - odd) * (rim + rows), 64), rim), :] = pair(near_ref[...])
    window[rim:rim + rows, :] = pair(own_ref[...])
    tracers = own_ref.shape[1]
    product = folded(dot(coarse2_ref[:, :width], window[...]))
    return product + dot(coarse2_ref[:, width:], window[:, :tracers])


def advance(coarse2_ref, far_ref, own_ref, near_ref, jump_ref, later_ref, *refs):
    state_ref, nfar_ref, nnear_ref, total_ref, window = refs[-5:]
    image = coarse_product(coarse2_ref, far_ref, own_ref, near_ref, window)
    state_ref[...] = image + (jump_ref[...] - later_ref[...])
    sides(state_ref, nfar_ref, nnear_ref, nfar_ref.shape[0])
    total_ref[...] = image if len(refs) == 5 else refs[0][...] + image


def finish(coarse2_ref, far_ref, own_ref, near_ref, image_ref, spread_ref, end_ref, out_ref, window):
    image = image_ref[...] + coarse_product(coarse2_ref, far_ref, own_ref, near_ref, window)
    split = pair(image)
    for b in range(end_ref.shape[0] // BS):
        rows = slice(b * BS, (b + 1) * BS)
        out_ref[rows, :] = end_ref[rows, :] + folded(dot(spread_ref[rows, :], split))


def swapped(far, near):
    count = lax.axis_size("tile")
    far = lax.ppermute(far, "tile", [(i, (i + 1 if i % 2 else i - 1) % count) for i in range(count)])
    near = lax.ppermute(near, "tile", [(i, i ^ 1) for i in range(count)])
    return far, near


def on_device(starts, sources, fine_ops, col_index, live_count, coarse_op, cell_map):
    first_state = starts[0]
    ops = fine_ops[0]
    rows, tracers = first_state.shape
    blocks, slots = ops.shape[:2]
    columns = col_index[0].T
    live = live_count
    coarse, reach = coarse_op.shape
    rim = (reach - coarse) // 2
    slices = lax.axis_size("tm")
    tiles = lax.axis_size("tile")
    window = pltpu.VMEM((rows + 2 * HALO, 2 * tracers), BF16)
    step_flops = 6 * rows * slots * BS * tracers
    coarse_flops = 6 * coarse * reach * tracers
    side = ((HALO, tracers), F32)
    coarse_rim = ((rim, tracers), F32)
    coarse_all = ((coarse, tracers), F32)

    far, near = call(ends, [side, side], [HBM], 0, 500_000, [pltpu.SemaphoreType.DMA((2,))])(kept(first_state))
    far, near = swapped(far, near)
    ops, own, sources = call(
        fetch, [(ops.shape, F32), ((rows, 2 * tracers), BF16), (sources.shape, F32)],
        [HBM] * 3, 0, 9_000_000, [pltpu.VMEM((rows, tracers), F32), pltpu.SemaphoreType.DMA((3,))],
    )(kept(ops), kept(first_state), kept(sources))

    step_in = [HBM] * 2 + [VMEM] * 5
    step_scratch = [pltpu.SMEM(columns.shape, jnp.int32), pltpu.SMEM(live.shape, jnp.int32), window,
                    pltpu.SemaphoreType.DMA((2,))]
    state, far, near, token = call(
        first_step, [((rows, 2 * tracers), BF16), side, side, ((8, tracers), F32)],
        step_in, step_flops, 6_000_000, step_scratch + [pltpu.VMEM((2 * HALO, tracers), F32)],
    )(kept(columns), kept(live), ops, own, far, near, sources)
    far, near = swapped(far, near)
    gather, spread, inverse, rstart, coarse2 = call(
        prepare,
        [((coarse, rows), BF16), ((rows, coarse), BF16), coarse_all, coarse_all, ((coarse, 2 * reach), BF16)],
        [HBM] * 2 + [VMEM, VMEM], 4 * coarse * rows * tracers, 6_000_000,
        [pltpu.VMEM((blocks, BS), jnp.int32), pltpu.VMEM((coarse, reach), F32), pltpu.SemaphoreType.DMA((2,))],
    )(kept(cell_map.reshape(-1, BS)), kept(coarse_op), own, token)
    following = lax.ppermute(rstart, "tm", [(1, 0)])
    later = lax.ppermute(rstart, "tm", [(i + 1, i) for i in range(1, slices - 1)])
    fine_end, jump, far, near = call(
        second_step, [((rows, tracers), F32), coarse_all, coarse_rim, coarse_rim],
        step_in + [VMEM] * 3, step_flops + 4 * coarse * rows * tracers, 8_000_000,
        step_scratch + [pltpu.VMEM((rows, 2 * tracers), BF16)],
    )(kept(columns), kept(live), ops, state, far, near, sources, gather, inverse, following)

    def to_slice(block, n, target):
        route = [((n - 1) * tiles + i, n * tiles + target(i) % tiles) for i in range(tiles)]
        return lax.ppermute(block, ("tm", "tile"), route)

    image = ()
    state = jump
    coarse_window = [pltpu.VMEM((reach, 2 * tracers), BF16)]
    for n in range(1, slices):
        far = to_slice(far, n, lambda i: i + 1 if i % 2 else i - 1)
        near = to_slice(near, n, lambda i: i ^ 1)
        own = to_slice(state, n, lambda i: i)
        if n < slices - 1:
            state, far, near, *image = call(
                advance, [coarse_all, coarse_rim, coarse_rim, coarse_all],
                [VMEM] * (6 + len(image)), coarse_flops, 2_000_000, coarse_window,
            )(coarse2, far, own, near, jump, later, *image)
        else:
            (result,) = call(
                finish, [((rows, tracers), F32)], [VMEM] * 7,
                coarse_flops + 4 * coarse * rows * tracers, 4_000_000, coarse_window,
            )(coarse2, far, own, near, *image, spread, fine_end)
    return result[None]


def solution(mesh):
    placed = (
        P("tm", "tile", None),
        P("tile", None),
        P("tm", "tile", None, None, None),
        P("tm", "tile", None),
        P("tm", "tile"),
        P("tile", None),
        P("tile"),
    )

    return jax.shard_map(on_device, mesh=mesh, in_specs=placed, out_specs=P("tm", "tile", None), check_vma=False)
```

time: 120 us -> 102 us (0.85)
  local copies, waits for them, and re-layouts: 14.9 us -> 0 us
  starting transfers between devices: 44.8 us -> 41.7 us
  waiting for transfers between devices: 47.1 us -> 44.1 us
  Pallas kernels: 11.9 us -> 14.5 us
    unnamed x35 -> x0, local copies, waits for them, and re-layouts: 13.1 us -> none
    ppermute x21, waiting for transfers between devices: 43.3 us -> 38.5 us  [to_slice(): return lax.ppermute(block, ('tm', 'tile'), route)]
    ppermute x5 -> x6, starting transfers between devices: 26.8 us -> 23.9 us  [the longest x2 17.4 us: swapped(): lax.ppermute(far, 'tile', [(i, (i + 1 if i % 2 else i - 1) % count) for i...]
    pallas_call x9 -> x11, Pallas kernels: 10.1 us -> 12.5 us  [the longest x6 3.38 us: on_device(): call(advance, [coarse_all, coarse_rim, coarse_rim, coarse_all], [VMEM] *...]
    ppermute x5 -> x6, waiting for transfers between devices: 3.78 us -> 5.58 us  [the longest x2 2.85 us: swapped(): near = lax.ppermute(near, 'tile', [(i, i ^ 1) for i in range(count)])]
    slice x1 -> x0, local copies, waits for them, and re-layouts: 1.69 us -> none  [on_device(): first_state[:HALO]]
  transfers between devices with their start and end apart: 26 -> 27, of which waited for: 5 -> 6; matrix products, arithmetic and copies ran while one was open for 0% -> 0% of each run, Pallas kernels for 4% -> 4%
where the time goes in v2:
time: 102 us; the launch traced here: 101 us
  waiting for transfers between devices  44.1 us (43%)
  starting transfers between devices  41.7 us (41%)
  Pallas kernels  14.5 us (14%)
    ppermute x21, waiting for transfers between devices, to_slice(): return lax.ppermute(block, ('tm', 'tile'), route)  38.5 us
    ppermute x21, starting transfers between devices, to_slice(): return lax.ppermute(block, ('tm', 'tile'), route)  17.8 us
    ppermute x2, starting transfers between devices, swapped(): lax.ppermute(far, 'tile', [(i, (i + 1 if i % 2 else i - 1) % count) for i...  17.4 us
    ppermute x2, starting transfers between devices, swapped(): near = lax.ppermute(near, 'tile', [(i, i ^ 1) for i in range(count)])  3.84 us
    pallas_call x6, Pallas kernels, on_device(): call(advance, [coarse_all, coarse_rim, coarse_rim, coarse_all], [VMEM] *...  3.38 us
    ppermute x2, waiting for transfers between devices, swapped(): near = lax.ppermute(near, 'tile', [(i, i ^ 1) for i in range(count)])  2.85 us
    ppermute x2, waiting for transfers between devices, swapped(): lax.ppermute(far, 'tile', [(i, (i + 1 if i % 2 else i - 1) % count) for i...  2.73 us
    pallas_call x1, Pallas kernels, on_device(): call(fetch, [(ops.shape, F32), ((rows, 2 * tracers), BF16), (sources.shap...  2.35 us
  transfers between devices with their start and end apart: 27, of which 6 were waited for; matrix products, arithmetic and copies ran while one was open for 0% of the time, Pallas kernels for 4%

profile of v2, /device:TPU:6, one launch (start us, length us, event | category | flops | bytes accessed | tf_op | source)
XLA Modules:
  0.0 100.7 jit_solution(12104526271455158280)
XLA Ops:
  0.0 1.0 shard_map.74
  1.0 13.9 %collective-permute-start = (f32[256,128]{1,0:T(8,128)S(1)}, f32[256,128]{1,0:T(8,128)S(1)}, u32[]{:S(2)}, u32[]{:S(2)}) collective-permute-start(f32[256,128]{1,0:T(8,128)S(1)} %get-tuple-element.49), channel_id=1, source_target_pairs={{0,63},{1,2},{2,1},{3,4},{4,3},{5,6},{6,5},{7,8},{8,7},{9,10},{10,... | collective-permute-start | bytes 393224 | tf_op jit(solution)/shard_map/ppermute | solution.py:213
  14.9 1.9 %collective-permute-start.1 = (f32[256,128]{1,0:T(8,128)S(1)}, f32[256,128]{1,0:T(8,128)S(1)}, u32[]{:S(2)}, u32[]{:S(2)}) collective-permute-start(f32[256,128]{1,0:T(8,128)S(1)} %get-tuple-element.50), channel_id=1, source_target_pairs={{0,1},{1,0},{2,3},{3,2},{4,5},{5,4},{6,7},{7,6},{8,9},{9,8},{10,11... | collective-permute-start | bytes 393224 | tf_op jit(solution)/shard_map/ppermute | solution.py:214
  16.8 2.3 %shard_map.73 = (f32[12,4,128,128]{3,2,1,0:T(8,128)S(1)}, bf16[1536,256]{1,0:T(8,128)(2,1)S(1)}, f32[1536,128]{1,0:T(8,128)S(1)}) custom-call(f32[12,4,128,128]{3,2,1,0:T(8,128)} %bitcast.9, f32[1536,128]{1,0:T(8,128)} %bitcast.8, f32[1536,128]{1,0:T(8,128)} %sources_ref.1), custom_call_target="tpu_custom_call" | custom-call | bytes 9000000 | tf_op jit(solution)/shard_map/pallas_call | solution.py:238
  19.1 0.0 collective-permute-done.far_ref
  19.1 2.6 %collective-permute-done.1.near_ref = f32[256,128]{1,0:T(8,128)S(1)} collective-permute-done((f32[256,128]{1,0:T(8,128)S(1)}, f32[256,128]{1,0:T(8,128)S(1)}, u32[]{:S(2)}, u32[]{:S(2)}) %collective-permute-start.1) | collective-permute-done | bytes 131104 | tf_op jit(solution)/shard_map/ppermute | solution.py:214
  21.7 1.7 %shard_map.75 = (bf16[1536,256]{1,0:T(8,128)(2,1)S(1)}, f32[256,128]{1,0:T(8,128)S(1)}, f32[256,128]{1,0:T(8,128)S(1)}, f32[8,128]{1,0:T(8,128)S(1)}) custom-call(s32[4,12]{1,0:T(4,128)} %bitcast.10, s32[1,12]{1,0:T(1,128)} %live_hbm.3, f32[12,4,128,128]{3,2,1,0:T(8,128)S(1)} %get-tuple-element.48.ops_ref, bf16[1536,256]{1,0:T(8,128)(2,1)S(1)} %get-tuple-element.47.own_ref, ...), custom_call_target="tpu_custom_call" | custom-call | flops 603979776 | bytes 6000000 | tf_op jit(solution)/shard_map/pallas_call | solution.py:246
  23.5 2.0 %shard_map.76 = (bf16[384,1536]{1,0:T(8,128)(2,1)S(1)}, bf16[1536,384]{1,0:T(8,128)(2,1)S(1)}, f32[384,128]{1,0:T(8,128)S(1)}, f32[384,128]{1,0:T(8,128)S(1)}, bf16[384,1536]{1,0:T(8,128)(2,1)S(1)}) custom-call(s32[12,128]{1,0:T(8,128)} %bitcast.12, f32[384,768]{1,0:T(8,128)} %coarse_hbm.1, bf16[1536,256]{1,0:T(8,128)(2,1)S(1)} %get-tuple-element.47.own_ref, ...), custom_call_target="tpu_custom_call" | custom-call | flops 301989888 | bytes 6000000 | tf_op jit(solution)/shard_map/pallas_call | solution.py:251
  25.5 0.7 collective-permute-start.4
  26.2 3.6 %collective-permute-start.2 = (f32[256,128]{1,0:T(8,128)S(1)}, f32[256,128]{1,0:T(8,128)S(1)}, u32[]{:S(2)}, u32[]{:S(2)}) collective-permute-start(f32[256,128]{1,0:T(8,128)S(1)} %get-tuple-element.55), channel_id=1, source_target_pairs={{0,63},{1,2},{2,1},{3,4},{4,3},{5,6},{6,5},{7,8},{8,7},{9,10},{10,... | collective-permute-start | bytes 393224 | tf_op jit(solution)/shard_map/ppermute | solution.py:213
  29.8 1.9 %collective-permute-start.3 = (f32[256,128]{1,0:T(8,128)S(1)}, f32[256,128]{1,0:T(8,128)S(1)}, u32[]{:S(2)}, u32[]{:S(2)}) collective-permute-start(f32[256,128]{1,0:T(8,128)S(1)} %get-tuple-element.56), channel_id=1, source_target_pairs={{0,1},{1,0},{2,3},{3,2},{4,5},{5,4},{6,7},{7,6},{8,9},{9,8},{10,11... | collective-permute-start | bytes 393224 | tf_op jit(solution)/shard_map/ppermute | solution.py:214
  31.7 1.9 %collective-permute-start.8 = (f32[384,128]{1,0:T(8,128)S(1)}, f32[384,128]{1,0:T(8,128)S(1)}, u32[]{:S(2)}, u32[]{:S(2)}) collective-permute-start(f32[384,128]{1,0:T(8,128)S(1)} %get-tuple-element.59), channel_id=1, source_target_pairs={{128,64},{192,128},{256,192},{320,256},{384,320},{448,384},{129,65... | collective-permute-start | bytes 589832 | tf_op jit(solution)/shard_map/ppermute | solution.py:258
  33.6 2.7 %collective-permute-done.2.far_ref = f32[256,128]{1,0:T(8,128)S(1)} collective-permute-done((f32[256,128]{1,0:T(8,128)S(1)}, f32[256,128]{1,0:T(8,128)S(1)}, u32[]{:S(2)}, u32[]{:S(2)}) %collective-permute-start.2) | collective-permute-done | bytes 131104 | tf_op jit(solution)/shard_map/ppermute | solution.py:213
  36.4 0.3 collective-permute-done.3.near_ref
  36.6 0.0 collective-permute-done.4.following_ref
  36.6 2.1 %shard_map.77 = (f32[1536,128]{1,0:T(8,128)S(1)}, f32[384,128]{1,0:T(8,128)S(1)}, f32[192,128]{1,0:T(8,128)S(1)}, f32[192,128]{1,0:T(8,128)S(1)}) custom-call(s32[4,12]{1,0:T(4,128)} %bitcast.11, s32[1,12]{1,0:T(1,128)} %live_hbm.3, f32[12,4,128,128]{3,2,1,0:T(8,128)S(1)} %get-tuple-element.48.ops_ref, bf16[1536,256]{1,0:T(8,128)(2,1)S(1)} %get-tuple-element.54.own_ref, ...), custom_call_target="tpu_custom_call" | custom-call | flops 905969664 | bytes 8000000 | tf_op jit(solution)/shard_map/pallas_call | solution.py:259
  38.7 0.7 collective-permute-start.6
  39.4 0.7 collective-permute-start.5
  40.1 0.7 collective-permute-start.7
  40.7 0.0 collective-permute-done.8.later_ref
  40.8 0.6 shard_map.78
  41.3 0.7 collective-permute-start.10
  42.0 0.7 collective-permute-start.9
  42.7 0.7 collective-permute-start.11
  43.4 0.6 shard_map.79
  44.0 0.7 collective-permute-start.13
  44.6 0.7 collective-permute-start.12
  45.3 0.7 collective-permute-start.14
  46.0 0.6 shard_map.80
  46.6 0.7 collective-permute-start.16
  47.3 0.7 collective-permute-start.15
  47.9 0.7 collective-permute-start.17
  48.7 0.6 shard_map.81
  49.2 0.7 collective-permute-start.19
  49.9 0.7 collective-permute-start.18
  50.6 0.7 collective-permute-start.20
  51.3 0.6 shard_map.82
  51.8 1.3 %collective-permute-start.22 = (f32[384,128]{1,0:T(8,128)S(1)}, f32[384,128]{1,0:T(8,128)S(1)}, u32[]{:S(2)}, u32[]{:S(2)}) collective-permute-start(f32[384,128]{1,0:T(8,128)S(1)} %get-tuple-element.80), channel_id=1, source_target_pairs={{320,384},{321,385},{322,386},{323,387},{324,388},{325,389},{326,3... | collective-permute-start | bytes 589832 | tf_op jit(solution)/shard_map/ppermute | solution.py:267
  53.1 1.3 %collective-permute-start.21 = (f32[192,128]{1,0:T(8,128)S(1)}, f32[192,128]{1,0:T(8,128)S(1)}, u32[]{:S(2)}, u32[]{:S(2)}) collective-permute-start(f32[192,128]{1,0:T(8,128)S(1)} %get-tuple-element.79), channel_id=1, source_target_pairs={{320,447},{321,386},{322,385},{323,388},{324,387},{325,390},{326,3... | collective-permute-start | bytes 294920 | tf_op jit(solution)/shard_map/ppermute | solution.py:267
  54.4 1.3 %collective-permute-start.23 = (f32[192,128]{1,0:T(8,128)S(1)}, f32[192,128]{1,0:T(8,128)S(1)}, u32[]{:S(2)}, u32[]{:S(2)}) collective-permute-start(f32[192,128]{1,0:T(8,128)S(1)} %get-tuple-element.81), channel_id=1, source_target_pairs={{320,385},{321,384},{322,387},{323,386},{324,389},{325,388},{326,3... | collective-permute-start | bytes 294920 | tf_op jit(solution)/shard_map/ppermute | solution.py:267
  55.7 36.3 %collective-permute-done.21.far_ref = f32[192,128]{1,0:T(8,128)S(1)} collective-permute-done((f32[192,128]{1,0:T(8,128)S(1)}, f32[192,128]{1,0:T(8,128)S(1)}, u32[]{:S(2)}, u32[]{:S(2)}) %collective-permute-start.21) | collective-permute-done | bytes 98336 | tf_op jit(solution)/shard_map/ppermute | solution.py:267
  92.1 0.6 shard_map.83
  92.6 1.3 %collective-permute-start.25 = (f32[384,128]{1,0:T(8,128)S(1)}, f32[384,128]{1,0:T(8,128)S(1)}, u32[]{:S(2)}, u32[]{:S(2)}) collective-permute-start(f32[384,128]{1,0:T(8,128)S(1)} %get-tuple-element.84), channel_id=1, source_target_pairs={{384,448},{385,449},{386,450},{387,451},{388,452},{389,453},{390,4... | collective-permute-start | bytes 589832 | tf_op jit(solution)/shard_map/ppermute | solution.py:267
  93.9 1.3 %collective-permute-start.24 = (f32[192,128]{1,0:T(8,128)S(1)}, f32[192,128]{1,0:T(8,128)S(1)}, u32[]{:S(2)}, u32[]{:S(2)}) collective-permute-start(f32[192,128]{1,0:T(8,128)S(1)} %get-tuple-element.83), channel_id=1, source_target_pairs={{384,511},{385,450},{386,449},{387,452},{388,451},{389,454},{390,4... | collective-permute-start | bytes 294920 | tf_op jit(solution)/shard_map/ppermute | solution.py:267
  95.2 1.3 %collective-permute-start.26 = (f32[192,128]{1,0:T(8,128)S(1)}, f32[192,128]{1,0:T(8,128)S(1)}, u32[]{:S(2)}, u32[]{:S(2)}) collective-permute-start(f32[192,128]{1,0:T(8,128)S(1)} %get-tuple-element.85), channel_id=1, source_target_pairs={{384,449},{385,448},{386,451},{387,450},{388,453},{389,452},{390,4... | collective-permute-start | bytes 294920 | tf_op jit(solution)/shard_map/ppermute | solution.py:267
  96.5 0.9 collective-permute-done.24.far_ref
  97.4 1.3 %collective-permute-done.26.near_ref = f32[192,128]{1,0:T(8,128)S(1)} collective-permute-done((f32[192,128]{1,0:T(8,128)S(1)}, f32[192,128]{1,0:T(8,128)S(1)}, u32[]{:S(2)}, u32[]{:S(2)}) %collective-permute-start.26) | collective-permute-done | bytes 98336 | tf_op jit(solution)/shard_map/ppermute | solution.py:267
  98.7 1.9 %shard_map.84 = f32[1536,128]{1,0:T(8,128)} custom-call(bf16[384,1536]{1,0:T(8,128)(2,1)S(1)} %get-tuple-element.53.coarse2_ref, f32[192,128]{1,0:T(8,128)S(1)} %collective-permute-done.24.far_ref, f32[384,128]{1,0:T(8,128)S(1)} %collective-permute-done.25.own_ref, f32[192,128]{1,0:T(8,128)S(1)} %collective-permute-done.26.near_ref, ...), custom_call_target="tpu_custom_call" | custom-call | flops 528482304 | bytes 4000000 | tf_op jit(solution)/shard_map/pallas_call | solution.py:282
  (18 shorter events, 0.0 us)
Async XLA Ops:
  1.0 18.1 %collective-permute-start = (f32[256,128]{1,0:T(8,128)S(1)}, f32[256,128]{1,0:T(8,128)S(1)}, u32[]{:S(2)}, u32[]{:S(2)}) collective-permute-start(f32[256,128]{1,0:T(8,128)S(1)} %get-tuple-element.49), channel_id=1, source_target_pairs={{0,63},{1,2},{2,1},{3,4},{4,3},{5,6},{6,5},{7,8},{8,7},{9,10},{10,... | collective-permute-start | bytes 393224 | tf_op jit(solution)/shard_map/ppermute | solution.py:213
  14.9 6.9 %collective-permute-start.1 = (f32[256,128]{1,0:T(8,128)S(1)}, f32[256,128]{1,0:T(8,128)S(1)}, u32[]{:S(2)}, u32[]{:S(2)}) collective-permute-start(f32[256,128]{1,0:T(8,128)S(1)} %get-tuple-element.50), channel_id=1, source_target_pairs={{0,1},{1,0},{2,3},{3,2},{4,5},{5,4},{6,7},{7,6},{8,9},{9,8},{10,11... | collective-permute-start | bytes 393224 | tf_op jit(solution)/shard_map/ppermute | solution.py:214
  25.5 11.1 %collective-permute-start.4 = (f32[384,128]{1,0:T(8,128)S(1)}, f32[384,128]{1,0:T(8,128)S(1)}, u32[]{:S(2)}, u32[]{:S(2)}) collective-permute-start(f32[384,128]{1,0:T(8,128)S(1)} %get-tuple-element.59), channel_id=1, source_target_pairs={{64,0},{65,1},{66,2},{67,3},{68,4},{69,5},{70,6},{71,7},{72,8},{73... | collective-permute-start | bytes 589832 | tf_op jit(solution)/shard_map/ppermute | solution.py:257
  26.2 10.2 %collective-permute-start.2 = (f32[256,128]{1,0:T(8,128)S(1)}, f32[256,128]{1,0:T(8,128)S(1)}, u32[]{:S(2)}, u32[]{:S(2)}) collective-permute-start(f32[256,128]{1,0:T(8,128)S(1)} %get-tuple-element.55), channel_id=1, source_target_pairs={{0,63},{1,2},{2,1},{3,4},{4,3},{5,6},{6,5},{7,8},{8,7},{9,10},{10,... | collective-permute-start | bytes 393224 | tf_op jit(solution)/shard_map/ppermute | solution.py:213
  29.8 6.9 %collective-permute-start.3 = (f32[256,128]{1,0:T(8,128)S(1)}, f32[256,128]{1,0:T(8,128)S(1)}, u32[]{:S(2)}, u32[]{:S(2)}) collective-permute-start(f32[256,128]{1,0:T(8,128)S(1)} %get-tuple-element.56), channel_id=1, source_target_pairs={{0,1},{1,0},{2,3},{3,2},{4,5},{5,4},{6,7},{7,6},{8,9},{9,8},{10,11... | collective-permute-start | bytes 393224 | tf_op jit(solution)/shard_map/ppermute | solution.py:214
  31.7 9.0 %collective-permute-start.8 = (f32[384,128]{1,0:T(8,128)S(1)}, f32[384,128]{1,0:T(8,128)S(1)}, u32[]{:S(2)}, u32[]{:S(2)}) collective-permute-start(f32[384,128]{1,0:T(8,128)S(1)} %get-tuple-element.59), channel_id=1, source_target_pairs={{128,64},{192,128},{256,192},{320,256},{384,320},{448,384},{129,65... | collective-permute-start | bytes 589832 | tf_op jit(solution)/shard_map/ppermute | solution.py:258
  38.7 2.1 %collective-permute-start.6 = (f32[384,128]{1,0:T(8,128)S(1)}, f32[384,128]{1,0:T(8,128)S(1)}, u32[]{:S(2)}, u32[]{:S(2)}) collective-permute-start(f32[384,128]{1,0:T(8,128)S(1)} %get-tuple-element.61.jump_ref), channel_id=1, source_target_pairs={{0,64},{1,65},{2,66},{3,67},{4,68},{5,69},{6,70},{7,71},{8,72},{9,... | collective-permute-start | bytes 589832 | tf_op jit(solution)/shard_map/ppermute | solution.py:267
  39.4 1.4 %collective-permute-start.5 = (f32[192,128]{1,0:T(8,128)S(1)}, f32[192,128]{1,0:T(8,128)S(1)}, u32[]{:S(2)}, u32[]{:S(2)}) collective-permute-start(f32[192,128]{1,0:T(8,128)S(1)} %get-tuple-element.60), channel_id=1, source_target_pairs={{0,127},{1,66},{2,65},{3,68},{4,67},{5,70},{6,69},{7,72},{8,71},{9... | collective-permute-start | bytes 294920 | tf_op jit(solution)/shard_map/ppermute | solution.py:267
  40.1 0.7 collective-permute-start.7
  41.3 2.1 %collective-permute-start.10 = (f32[384,128]{1,0:T(8,128)S(1)}, f32[384,128]{1,0:T(8,128)S(1)}, u32[]{:S(2)}, u32[]{:S(2)}) collective-permute-start(f32[384,128]{1,0:T(8,128)S(1)} %get-tuple-element.64), channel_id=1, source_target_pairs={{64,128},{65,129},{66,130},{67,131},{68,132},{69,133},{70,134},{71... | collective-permute-start | bytes 589832 | tf_op jit(solution)/shard_map/ppermute | solution.py:267
  42.0 1.4 %collective-permute-start.9 = (f32[192,128]{1,0:T(8,128)S(1)}, f32[192,128]{1,0:T(8,128)S(1)}, u32[]{:S(2)}, u32[]{:S(2)}) collective-permute-start(f32[192,128]{1,0:T(8,128)S(1)} %get-tuple-element.63), channel_id=1, source_target_pairs={{64,191},{65,130},{66,129},{67,132},{68,131},{69,134},{70,133},{71... | collective-permute-start | bytes 294920 | tf_op jit(solution)/shard_map/ppermute | solution.py:267
  42.7 0.7 collective-permute-start.11
  44.0 2.1 %collective-permute-start.13 = (f32[384,128]{1,0:T(8,128)S(1)}, f32[384,128]{1,0:T(8,128)S(1)}, u32[]{:S(2)}, u32[]{:S(2)}) collective-permute-start(f32[384,128]{1,0:T(8,128)S(1)} %get-tuple-element.68), channel_id=1, source_target_pairs={{128,192},{129,193},{130,194},{131,195},{132,196},{133,197},{134,1... | collective-permute-start | bytes 589832 | tf_op jit(solution)/shard_map/ppermute | solution.py:267
  44.6 1.4 %collective-permute-start.12 = (f32[192,128]{1,0:T(8,128)S(1)}, f32[192,128]{1,0:T(8,128)S(1)}, u32[]{:S(2)}, u32[]{:S(2)}) collective-permute-start(f32[192,128]{1,0:T(8,128)S(1)} %get-tuple-element.67), channel_id=1, source_target_pairs={{128,255},{129,194},{130,193},{131,196},{132,195},{133,198},{134,1... | collective-permute-start | bytes 294920 | tf_op jit(solution)/shard_map/ppermute | solution.py:267
  45.3 0.7 collective-permute-start.14
  46.6 2.1 %collective-permute-start.16 = (f32[384,128]{1,0:T(8,128)S(1)}, f32[384,128]{1,0:T(8,128)S(1)}, u32[]{:S(2)}, u32[]{:S(2)}) collective-permute-start(f32[384,128]{1,0:T(8,128)S(1)} %get-tuple-element.72), channel_id=1, source_target_pairs={{192,256},{193,257},{194,258},{195,259},{196,260},{197,261},{198,2... | collective-permute-start | bytes 589832 | tf_op jit(solution)/shard_map/ppermute | solution.py:267
  47.3 1.4 %collective-permute-start.15 = (f32[192,128]{1,0:T(8,128)S(1)}, f32[192,128]{1,0:T(8,128)S(1)}, u32[]{:S(2)}, u32[]{:S(2)}) collective-permute-start(f32[192,128]{1,0:T(8,128)S(1)} %get-tuple-element.71), channel_id=1, source_target_pairs={{192,319},{193,258},{194,257},{195,260},{196,259},{197,262},{198,2... | collective-permute-start | bytes 294920 | tf_op jit(solution)/shard_map/ppermute | solution.py:267
  47.9 0.7 collective-permute-start.17
  49.2 2.1 %collective-permute-start.19 = (f32[384,128]{1,0:T(8,128)S(1)}, f32[384,128]{1,0:T(8,128)S(1)}, u32[]{:S(2)}, u32[]{:S(2)}) collective-permute-start(f32[384,128]{1,0:T(8,128)S(1)} %get-tuple-element.76), channel_id=1, source_target_pairs={{256,320},{257,321},{258,322},{259,323},{260,324},{261,325},{262,3... | collective-permute-start | bytes 589832 | tf_op jit(solution)/shard_map/ppermute | solution.py:267
  49.9 1.4 %collective-permute-start.18 = (f32[192,128]{1,0:T(8,128)S(1)}, f32[192,128]{1,0:T(8,128)S(1)}, u32[]{:S(2)}, u32[]{:S(2)}) collective-permute-start(f32[192,128]{1,0:T(8,128)S(1)} %get-tuple-element.75), channel_id=1, source_target_pairs={{256,383},{257,322},{258,321},{259,324},{260,323},{261,326},{262,3... | collective-permute-start | bytes 294920 | tf_op jit(solution)/shard_map/ppermute | solution.py:267
  50.6 0.7 collective-permute-start.20
  51.8 40.2 %collective-permute-start.22 = (f32[384,128]{1,0:T(8,128)S(1)}, f32[384,128]{1,0:T(8,128)S(1)}, u32[]{:S(2)}, u32[]{:S(2)}) collective-permute-start(f32[384,128]{1,0:T(8,128)S(1)} %get-tuple-element.80), channel_id=1, source_target_pairs={{320,384},{321,385},{322,386},{323,387},{324,388},{325,389},{326,3... | collective-permute-start | bytes 589832 | tf_op jit(solution)/shard_map/ppermute | solution.py:267
  53.1 38.9 %collective-permute-start.21 = (f32[192,128]{1,0:T(8,128)S(1)}, f32[192,128]{1,0:T(8,128)S(1)}, u32[]{:S(2)}, u32[]{:S(2)}) collective-permute-start(f32[192,128]{1,0:T(8,128)S(1)} %get-tuple-element.79), channel_id=1, source_target_pairs={{320,447},{321,386},{322,385},{323,388},{324,387},{325,390},{326,3... | collective-permute-start | bytes 294920 | tf_op jit(solution)/shard_map/ppermute | solution.py:267
  54.4 37.6 %collective-permute-start.23 = (f32[192,128]{1,0:T(8,128)S(1)}, f32[192,128]{1,0:T(8,128)S(1)}, u32[]{:S(2)}, u32[]{:S(2)}) collective-permute-start(f32[192,128]{1,0:T(8,128)S(1)} %get-tuple-element.81), channel_id=1, source_target_pairs={{320,385},{321,384},{322,387},{323,386},{324,389},{325,388},{326,3... | collective-permute-start | bytes 294920 | tf_op jit(solution)/shard_map/ppermute | solution.py:267
  92.6 6.1 %collective-permute-start.25 = (f32[384,128]{1,0:T(8,128)S(1)}, f32[384,128]{1,0:T(8,128)S(1)}, u32[]{:S(2)}, u32[]{:S(2)}) collective-permute-start(f32[384,128]{1,0:T(8,128)S(1)} %get-tuple-element.84), channel_id=1, source_target_pairs={{384,448},{385,449},{386,450},{387,451},{388,452},{389,453},{390,4... | collective-permute-start | bytes 589832 | tf_op jit(solution)/shard_map/ppermute | solution.py:267
  93.9 3.5 %collective-permute-start.24 = (f32[192,128]{1,0:T(8,128)S(1)}, f32[192,128]{1,0:T(8,128)S(1)}, u32[]{:S(2)}, u32[]{:S(2)}) collective-permute-start(f32[192,128]{1,0:T(8,128)S(1)} %get-tuple-element.83), channel_id=1, source_target_pairs={{384,511},{385,450},{386,449},{387,452},{388,451},{389,454},{390,4... | collective-permute-start | bytes 294920 | tf_op jit(solution)/shard_map/ppermute | solution.py:267
  95.2 3.5 %collective-permute-start.26 = (f32[192,128]{1,0:T(8,128)S(1)}, f32[192,128]{1,0:T(8,128)S(1)}, u32[]{:S(2)}, u32[]{:S(2)}) collective-permute-start(f32[192,128]{1,0:T(8,128)S(1)} %get-tuple-element.85), channel_id=1, source_target_pairs={{384,449},{385,448},{386,451},{387,450},{388,453},{389,452},{390,4... | collective-permute-start | bytes 294920 | tf_op jit(solution)/shard_map/ppermute | solution.py:267
